TPU v7x, 256 devices: a whole 4x4x8 slice. The times are simulated.
256 devices in a mesh: seq: 64 (over x_hi, y, z), ch: 4 (over x_lo, core).
Axes of the slice: x: 4 (x_hi: 2, x_lo: 2; x = x_hi * 2 + x_lo), y: 4, z: 8, core: 2. Of those that a mesh axis runs over, the one named last changes fastest.
Arguments:
- signal: bfloat16 [16384, 2048], P('seq', 'ch'), may hold values from -6 to 6
- gate_in: bfloat16 [16384, 2048], P('seq', 'ch'), may hold values from -6 to 6
- skip_gain: float32 [2048], P('ch'), may hold values from -1 to 1
- decay: float32 [2048], P('ch'), may hold values from 6.1035156e-05 to 0.0009765625
- pos_weight1: float32 [33, 64], replicated, may hold values from -16 to 16
- pos_bias1: float32 [64], replicated, may hold values from -4 to 4
- pos_weight2: float32 [64, 64], replicated, may hold values from -0.75 to 0.75
- pos_bias2: float32 [64], replicated, may hold values from -4 to 4
- filt_hi: bfloat16 [64, 2048], P(None, 'ch'), may hold values from -0.75 to 0.75
- filt_fix: int32 [64, 2048], P(None, 'ch'), may hold values from -128 to 127
- out_weight: bfloat16 [2048, 4096], P('ch'), may hold values from -0.125 to 0.125
Outputs:
- mixed: bfloat16 [16384, 4096], P('seq', 'ch')
All inputs are finite; a program needn't handle non-finite values.
Results may differ from a plain program's by a relative error of at most 0.005.
Values sent between devices are 32-bit elements; how exact they have to be, the bound alone decides.
A program may use at most 128 MiB of HBM per device.

v0:
```python
import math

import jax
import jax.numpy as jnp
from jax import lax
from jax.sharding import PartitionSpec as P

precise = lax.Precision.HIGHEST


def from_partner(value, axis, bit):
    mask = 2**bit
    pairs = [(source, source ^ mask) for source in range(lax.axis_size(axis))]
    return lax.ppermute(value, axis, pairs)


def filter_rows(
    positions, seq_len, pos_weight1, pos_bias1, pos_weight2, pos_bias2, filter_weight, decay
):
    pos_float = positions.astype(jnp.float32)
    harmonics = jnp.arange(1, (pos_weight1.shape[0] - 1) // 2 + 1, dtype=jnp.int32)
    phases = (positions[:, None] * harmonics[None, :] % seq_len).astype(jnp.float32) * (
        2.0 * math.pi / seq_len
    )
    features = jnp.concatenate(
        [(pos_float / seq_len)[:, None], jnp.cos(phases), jnp.sin(phases)], axis=1
    )
    hidden_one = jnp.sin(jnp.dot(features, pos_weight1, precision=precise) + pos_bias1)
    hidden_two = jnp.sin(jnp.dot(hidden_one, pos_weight2, precision=precise) + pos_bias2)
    raw_rows = jnp.dot(hidden_two, filter_weight, precision=precise)
    envelope = (
        jnp.exp(-decay[None, :] * pos_float[:, None])
        * jnp.sqrt(2.0 * decay + 1.0 / seq_len)[None, :]
    )
    return raw_rows * envelope


def phasor(numerator, modulus, sign_val):
    angles = (numerator % modulus).astype(jnp.float32) * (sign_val * 2.0 * math.pi / modulus)
    return (jnp.cos(angles), jnp.sin(angles))


def complex_mul(left_real, left_imag, right_real, right_imag):
    return (
        left_real * right_real - left_imag * right_imag,
        left_real * right_imag + left_imag * right_real,
    )


def split_halves(values, first_row, seq_len):
    offsets = jnp.arange(values.shape[0], dtype=jnp.int32)
    cos_part, sin_part = phasor(first_row + offsets, 2 * seq_len, -1.0)
    real_part = jnp.stack([values, values * cos_part[:, None]])
    imag_part = jnp.stack([jnp.zeros_like(values), values * sin_part[:, None]])
    return (real_part, imag_part)


def local_forward(real_part, imag_part):
    rows = real_part.shape[1]
    offsets = jnp.arange(rows, dtype=jnp.int32)
    cos_part, sin_part = phasor(offsets[:, None] * offsets[None, :], rows, -1.0)
    out_real = jnp.einsum("bj,hjc->hbc", cos_part, real_part, precision=precise) - jnp.einsum(
        "bj,hjc->hbc", sin_part, imag_part, precision=precise
    )
    out_imag = jnp.einsum("bj,hjc->hbc", cos_part, imag_part, precision=precise) + jnp.einsum(
        "bj,hjc->hbc", sin_part, real_part, precision=precise
    )
    return (out_real, out_imag)


def local_inverse(real_part, imag_part):
    rows = real_part.shape[1]
    offsets = jnp.arange(rows, dtype=jnp.int32)
    cos_part, sin_part = phasor(offsets[:, None] * offsets[None, :], rows, 1.0)
    out_real = jnp.einsum("jb,hbc->hjc", cos_part, real_part, precision=precise) - jnp.einsum(
        "jb,hbc->hjc", sin_part, imag_part, precision=precise
    )
    out_imag = jnp.einsum("jb,hbc->hjc", cos_part, imag_part, precision=precise) + jnp.einsum(
        "jb,hbc->hjc", sin_part, real_part, precision=precise
    )
    return (out_real / rows, out_imag / rows)


def forward_bits(real_part, imag_part, seq_rank, seq_len):
    tok_rows = real_part.shape[1]
    dev_count = lax.axis_size("seq")
    level_count = dev_count.bit_length() - 1
    offsets = jnp.arange(tok_rows, dtype=jnp.int32)
    for section_num in range(level_count):
        bit_pos = level_count - 1 - section_num
        sub_len = seq_len >> section_num
        group_size = dev_count >> section_num + 1
        upper_half = seq_rank >> bit_pos & 1 == 1
        recv_real, recv_imag = from_partner((real_part, imag_part), "seq", bit_pos)
        cos_part, sin_part = phasor(seq_rank % group_size * tok_rows + offsets, sub_len, -1.0)
        diff_real, diff_imag = complex_mul(
            recv_real - real_part,
            recv_imag - imag_part,
            cos_part[None, :, None],
            sin_part[None, :, None],
        )
        real_part = jnp.where(upper_half, diff_real, real_part + recv_real)
        imag_part = jnp.where(upper_half, diff_imag, imag_part + recv_imag)
    return (real_part, imag_part)


def inverse_bits(real_part, imag_part, seq_rank, seq_len):
    tok_rows = real_part.shape[1]
    dev_count = lax.axis_size("seq")
    level_count = dev_count.bit_length() - 1
    offsets = jnp.arange(tok_rows, dtype=jnp.int32)
    for section_num in reversed(range(level_count)):
        bit_pos = level_count - 1 - section_num
        sub_len = seq_len >> section_num
        group_size = dev_count >> section_num + 1
        upper_half = seq_rank >> bit_pos & 1 == 1
        cos_part, sin_part = phasor(seq_rank % group_size * tok_rows + offsets, sub_len, 1.0)
        turned_real, turned_imag = complex_mul(
            real_part, imag_part, cos_part[None, :, None], sin_part[None, :, None]
        )
        send_real = jnp.where(upper_half, turned_real, real_part)
        send_imag = jnp.where(upper_half, turned_imag, imag_part)
        recv_real, recv_imag = from_partner((send_real, send_imag), "seq", bit_pos)
        real_part = jnp.where(upper_half, recv_real - send_real, send_real + recv_real) * 0.5
        imag_part = jnp.where(upper_half, recv_imag - send_imag, send_imag + recv_imag) * 0.5
    return (real_part, imag_part)


def transform(real_part, imag_part, seq_rank, seq_len):
    real_part, imag_part = forward_bits(real_part, imag_part, seq_rank, seq_len)
    return local_forward(real_part, imag_part)


def shards(
    signal,
    gate_in,
    skip_gain,
    decay,
    pos_weight1,
    pos_bias1,
    pos_weight2,
    pos_bias2,
    filt_hi,
    filt_fix,
    out_weight,
):
    tok_rows = signal.shape[0]
    dev_count = lax.axis_size("seq")
    seq_rank = lax.axis_index("seq")
    seq_len = tok_rows * dev_count
    first_row = seq_rank * tok_rows
    offsets = jnp.arange(tok_rows, dtype=jnp.int32)
    filter_weight = filt_hi.astype(jnp.float32) + filt_fix.astype(jnp.float32) * 2.0 ** (-11)
    values = signal.astype(jnp.float32)
    half_real, half_imag = split_halves(values, first_row, seq_len)
    sig_real, sig_imag = transform(half_real, half_imag, seq_rank, seq_len)
    own_filters = filter_rows(
        first_row + offsets,
        seq_len,
        pos_weight1,
        pos_bias1,
        pos_weight2,
        pos_bias2,
        filter_weight,
        decay,
    )
    fil_half_real, fil_half_imag = split_halves(own_filters, first_row, seq_len)
    fil_real, fil_imag = transform(fil_half_real, fil_half_imag, seq_rank, seq_len)
    prod_real, prod_imag = complex_mul(sig_real, sig_imag, fil_real, fil_imag)
    prod_real, prod_imag = local_inverse(prod_real, prod_imag)
    prod_real, prod_imag = inverse_bits(prod_real, prod_imag, seq_rank, seq_len)
    cos_part, sin_part = phasor(first_row + offsets, 2 * seq_len, 1.0)
    convolved = 0.5 * (
        prod_real[0] + prod_real[1] * cos_part[:, None] - prod_imag[1] * sin_part[:, None]
    )
    gated = (gate_in.astype(jnp.float32) * (convolved + skip_gain[None, :] * values)).astype(
        jnp.bfloat16
    )
    partial_out = jnp.dot(gated, out_weight, preferred_element_type=jnp.float32)
    return lax.psum_scatter(partial_out, "ch", scatter_dimension=1, tiled=True).astype(jnp.bfloat16)


def solution(mesh):
    return jax.shard_map(
        shards,
        mesh=mesh,
        in_specs=(
            P("seq", "ch"),
            P("seq", "ch"),
            P("ch"),
            P("ch"),
            P(),
            P(),
            P(),
            P(),
            P(None, "ch"),
            P(None, "ch"),
            P("ch", None),
        ),
        out_specs=P("seq", "ch"),
        check_vma=False,
    )
```

profile of v0, /device:TPU:1, one launch (start us, length us, event | category | flops | bytes accessed | tf_op | source)
XLA Modules:
  0.0 1256.1 jit_solution(15560797061108633202)
XLA Ops:
  14.0 3.6 collective-permute-start.12
  19.9 3.0 collective-permute-start.1
  24.1 15.7 %collective-permute-done.12 = f32[2,256,512]{2,1,0:T(8,128)} collective-permute-done((f32[2,256,512]{2,1,0:T(8,128)}, f32[2,256,512]{2,1,0:T(8,128)}, u32[]{:S(2)}, u32[]{:S(2)}) %collective-permute-start.12) | collective-permute-done | bytes 1048608 | tf_op jit(solution)/shard_map/ppermute | solution.py:14
  39.8 22.5 %collective-permute-done = f32[2,256,512]{2,1,0:T(8,128)} collective-permute-done((f32[2,256,512]{2,1,0:T(8,128)}, f32[2,256,512]{2,1,0:T(8,128)}, u32[]{:S(2)}, u32[]{:S(2)}) %collective-permute-start) | collective-permute-done | bytes 1048608 | tf_op jit(solution)/shard_map/ppermute | solution.py:14
  62.2 22.5 %collective-permute-done.1 = f32[2,256,512]{2,1,0:T(8,128)} collective-permute-done((f32[2,256,512]{2,1,0:T(8,128)}, f32[2,256,512]{2,1,0:T(8,128)}, u32[]{:S(2)}, u32[]{:S(2)}) %collective-permute-start.1) | collective-permute-done | bytes 1048608 | tf_op jit(solution)/shard_map/ppermute | solution.py:14
  84.7 22.5 %collective-permute-done.13 = f32[2,256,512]{2,1,0:T(8,128)} collective-permute-done((f32[2,256,512]{2,1,0:T(8,128)}, f32[2,256,512]{2,1,0:T(8,128)}, u32[]{:S(2)}, u32[]{:S(2)}) %collective-permute-start.13) | collective-permute-done | bytes 1048608 | tf_op jit(solution)/shard_map/ppermute | solution.py:14
  107.2 5.1 add_select_fusion.20
  112.2 3.8 collective-permute-start.14
  116.1 2.9 collective-permute-start.2
  119.2 18.9 %collective-permute-done.14 = f32[2,256,512]{2,1,0:T(8,128)S(1)} collective-permute-done((f32[2,256,512]{2,1,0:T(8,128)}, f32[2,256,512]{2,1,0:T(8,128)S(1)}, u32[]{:S(2)}, u32[]{:S(2)}) %collective-permute-start.14) | collective-permute-done | bytes 1048608 | tf_op jit(solution)/shard_map/ppermute | solution.py:14
  138.1 22.5 %collective-permute-done.15 = f32[2,256,512]{2,1,0:T(8,128)S(1)} collective-permute-done((f32[2,256,512]{2,1,0:T(8,128)}, f32[2,256,512]{2,1,0:T(8,128)S(1)}, u32[]{:S(2)}, u32[]{:S(2)}) %collective-permute-start.15) | collective-permute-done | bytes 1048608 | tf_op jit(solution)/shard_map/ppermute | solution.py:14
  160.6 22.5 %collective-permute-done.2 = f32[2,256,512]{2,1,0:T(8,128)S(1)} collective-permute-done((f32[2,256,512]{2,1,0:T(8,128)}, f32[2,256,512]{2,1,0:T(8,128)S(1)}, u32[]{:S(2)}, u32[]{:S(2)}) %collective-permute-start.2) | collective-permute-done | bytes 1048608 | tf_op jit(solution)/shard_map/ppermute | solution.py:14
  183.0 22.6 %collective-permute-done.3 = f32[2,256,512]{2,1,0:T(8,128)} collective-permute-done((f32[2,256,512]{2,1,0:T(8,128)}, f32[2,256,512]{2,1,0:T(8,128)}, u32[]{:S(2)}, u32[]{:S(2)}) %collective-permute-start.3) | collective-permute-done | bytes 1048608 | tf_op jit(solution)/shard_map/ppermute | solution.py:14
  205.6 5.8 add_select_fusion.18
  214.6 19.3 %collective-permute-done.16 = f32[2,256,512]{2,1,0:T(8,128)} collective-permute-done((f32[2,256,512]{2,1,0:T(8,128)S(1)}, f32[2,256,512]{2,1,0:T(8,128)}, u32[]{:S(2)}, u32[]{:S(2)}) %collective-permute-start.16) | collective-permute-done | bytes 1048608 | tf_op jit(solution)/shard_map/ppermute | solution.py:14
  233.9 22.5 %collective-permute-done.17 = f32[2,256,512]{2,1,0:T(8,128)} collective-permute-done((f32[2,256,512]{2,1,0:T(8,128)S(1)}, f32[2,256,512]{2,1,0:T(8,128)}, u32[]{:S(2)}, u32[]{:S(2)}) %collective-permute-start.17) | collective-permute-done | bytes 1048608 | tf_op jit(solution)/shard_map/ppermute | solution.py:14
  256.3 22.5 %collective-permute-done.4 = f32[2,256,512]{2,1,0:T(8,128)} collective-permute-done((f32[2,256,512]{2,1,0:T(8,128)S(1)}, f32[2,256,512]{2,1,0:T(8,128)}, u32[]{:S(2)}, u32[]{:S(2)}) %collective-permute-start.4) | collective-permute-done | bytes 1048608 | tf_op jit(solution)/shard_map/ppermute | solution.py:14
  278.8 22.5 %collective-permute-done.5 = f32[2,256,512]{2,1,0:T(8,128)} collective-permute-done((f32[2,256,512]{2,1,0:T(8,128)}, f32[2,256,512]{2,1,0:T(8,128)}, u32[]{:S(2)}, u32[]{:S(2)}) %collective-permute-start.5) | collective-permute-done | bytes 1048608 | tf_op jit(solution)/shard_map/ppermute | solution.py:14
  301.3 5.6 add_select_fusion.16
  306.9 6.7 collective-permute-start.18
  313.6 5.3 collective-permute-start.6
  319.1 19.5 %collective-permute-done.18 = f32[2,256,512]{2,1,0:T(8,128)S(1)} collective-permute-done((f32[2,256,512]{2,1,0:T(8,128)}, f32[2,256,512]{2,1,0:T(8,128)S(1)}, u32[]{:S(2)}, u32[]{:S(2)}) %collective-permute-start.18) | collective-permute-done | bytes 1048608 | tf_op jit(solution)/shard_map/ppermute | solution.py:14
  338.5 32.1 %collective-permute-done.19 = f32[2,256,512]{2,1,0:T(8,128)S(1)} collective-permute-done((f32[2,256,512]{2,1,0:T(8,128)}, f32[2,256,512]{2,1,0:T(8,128)S(1)}, u32[]{:S(2)}, u32[]{:S(2)}) %collective-permute-start.19) | collective-permute-done | bytes 1048608 | tf_op jit(solution)/shard_map/ppermute | solution.py:14
  370.6 40.0 %collective-permute-done.6 = f32[2,256,512]{2,1,0:T(8,128)S(1)} collective-permute-done((f32[2,256,512]{2,1,0:T(8,128)}, f32[2,256,512]{2,1,0:T(8,128)S(1)}, u32[]{:S(2)}, u32[]{:S(2)}) %collective-permute-start.6) | collective-permute-done | bytes 1048608 | tf_op jit(solution)/shard_map/ppermute | solution.py:14
  410.7 50.0 %collective-permute-done.7 = f32[2,256,512]{2,1,0:T(8,128)} collective-permute-done((f32[2,256,512]{2,1,0:T(8,128)}, f32[2,256,512]{2,1,0:T(8,128)}, u32[]{:S(2)}, u32[]{:S(2)}) %collective-permute-start.7) | collective-permute-done | bytes 1048608 | tf_op jit(solution)/shard_map/ppermute | solution.py:14
  460.7 5.8 add_select_fusion.14
  466.5 35.3 %collective-permute-start.20 = (f32[2,256,512]{2,1,0:T(8,128)S(1)}, f32[2,256,512]{2,1,0:T(8,128)}, u32[]{:S(2)}, u32[]{:S(2)}) collective-permute-start(f32[2,256,512]{2,1,0:T(8,128)S(1)} %get-tuple-element.20), channel_id=1, source_target_pairs={{0,8},{4,12},{8,0},{12,4},{16,24},{20,28},{24,16},{28,20},{32,40},... | collective-permute-start | bytes 3145736 | tf_op jit(solution)/shard_map/ppermute | solution.py:14
  501.9 2.3 collective-permute-start.8
  504.3 110.7 %collective-permute-done.20 = f32[2,256,512]{2,1,0:T(8,128)} collective-permute-done((f32[2,256,512]{2,1,0:T(8,128)S(1)}, f32[2,256,512]{2,1,0:T(8,128)}, u32[]{:S(2)}, u32[]{:S(2)}) %collective-permute-start.20) | collective-permute-done | bytes 1048608 | tf_op jit(solution)/shard_map/ppermute | solution.py:14
  615.0 22.5 %collective-permute-done.21 = f32[2,256,512]{2,1,0:T(8,128)} collective-permute-done((f32[2,256,512]{2,1,0:T(8,128)S(1)}, f32[2,256,512]{2,1,0:T(8,128)}, u32[]{:S(2)}, u32[]{:S(2)}) %collective-permute-start.21) | collective-permute-done | bytes 1048608 | tf_op jit(solution)/shard_map/ppermute | solution.py:14
  637.5 22.5 %collective-permute-done.8 = f32[2,256,512]{2,1,0:T(8,128)} collective-permute-done((f32[2,256,512]{2,1,0:T(8,128)S(1)}, f32[2,256,512]{2,1,0:T(8,128)}, u32[]{:S(2)}, u32[]{:S(2)}) %collective-permute-start.8) | collective-permute-done | bytes 1048608 | tf_op jit(solution)/shard_map/ppermute | solution.py:14
  660.0 22.5 %collective-permute-done.9 = f32[2,256,512]{2,1,0:T(8,128)} collective-permute-done((f32[2,256,512]{2,1,0:T(8,128)}, f32[2,256,512]{2,1,0:T(8,128)}, u32[]{:S(2)}, u32[]{:S(2)}) %collective-permute-start.9) | collective-permute-done | bytes 1048608 | tf_op jit(solution)/shard_map/ppermute | solution.py:14
  682.4 5.6 add_select_fusion.12
  691.5 20.5 %collective-permute-done.10 = f32[2,256,512]{2,1,0:T(8,128)S(1)} collective-permute-done((f32[2,256,512]{2,1,0:T(8,128)}, f32[2,256,512]{2,1,0:T(8,128)S(1)}, u32[]{:S(2)}, u32[]{:S(2)}) %collective-permute-start.10) | collective-permute-done | bytes 1048608 | tf_op jit(solution)/shard_map/ppermute | solution.py:14
  712.0 22.5 %collective-permute-done.11 = f32[2,256,512]{2,1,0:T(8,128)S(1)} collective-permute-done((f32[2,256,512]{2,1,0:T(8,128)}, f32[2,256,512]{2,1,0:T(8,128)S(1)}, u32[]{:S(2)}, u32[]{:S(2)}) %collective-permute-start.11) | collective-permute-done | bytes 1048608 | tf_op jit(solution)/shard_map/ppermute | solution.py:14
  734.4 22.5 %collective-permute-done.22 = f32[2,256,512]{2,1,0:T(8,128)S(1)} collective-permute-done((f32[2,256,512]{2,1,0:T(8,128)}, f32[2,256,512]{2,1,0:T(8,128)S(1)}, u32[]{:S(2)}, u32[]{:S(2)}) %collective-permute-start.22) | collective-permute-done | bytes 1048608 | tf_op jit(solution)/shard_map/ppermute | solution.py:14
  756.9 22.6 %collective-permute-done.23 = f32[2,256,512]{2,1,0:T(8,128)} collective-permute-done((f32[2,256,512]{2,1,0:T(8,128)}, f32[2,256,512]{2,1,0:T(8,128)}, u32[]{:S(2)}, u32[]{:S(2)}) %collective-permute-start.23) | collective-permute-done | bytes 1048608 | tf_op jit(solution)/shard_map/ppermute | solution.py:14
  779.5 3.7 add_select_fusion.10
  783.1 2.7 fusion.26
  785.8 2.7 fusion.30
  788.5 2.7 convolution_add_fusion.1
  791.2 2.8 fusion.32
  794.1 2.7 fusion.28
  796.7 2.7 convolution_subtract_fusion.2
  799.4 2.7 convolution_subtract_fusion.1
  802.1 2.9 multiply_add_fusion
  811.5 2.5 select_bitcast_fusion
  815.6 21.3 %collective-permute-done.24 = f32[2,256,512]{2,1,0:T(8,128)S(1)} collective-permute-done((f32[2,256,512]{2,1,0:T(8,128)S(1)}, f32[2,256,512]{2,1,0:T(8,128)S(1)}, u32[]{:S(2)}, u32[]{:S(2)}) %collective-permute-start.24) | collective-permute-done | bytes 1048608 | tf_op jit(solution)/shard_map/ppermute | solution.py:14
  836.9 22.5 %collective-permute-done.25 = f32[2,256,512]{2,1,0:T(8,128)S(1)} collective-permute-done((f32[2,256,512]{2,1,0:T(8,128)S(1)}, f32[2,256,512]{2,1,0:T(8,128)S(1)}, u32[]{:S(2)}, u32[]{:S(2)}) %collective-permute-start.25) | collective-permute-done | bytes 1048608 | tf_op jit(solution)/shard_map/ppermute | solution.py:14
  862.5 68.5 %collective-permute-done.26 = f32[2,256,512]{2,1,0:T(8,128)S(1)} collective-permute-done((f32[2,256,512]{2,1,0:T(8,128)S(1)}, f32[2,256,512]{2,1,0:T(8,128)S(1)}, u32[]{:S(2)}, u32[]{:S(2)}) %collective-permute-start.26) | collective-permute-done | bytes 1048608 | tf_op jit(solution)/shard_map/ppermute | solution.py:14
  931.0 22.5 %collective-permute-done.27 = f32[2,256,512]{2,1,0:T(8,128)S(1)} collective-permute-done((f32[2,256,512]{2,1,0:T(8,128)S(1)}, f32[2,256,512]{2,1,0:T(8,128)S(1)}, u32[]{:S(2)}, u32[]{:S(2)}) %collective-permute-start.27) | collective-permute-done | bytes 1048608 | tf_op jit(solution)/shard_map/ppermute | solution.py:14
  954.1 3.8 collective-permute-start.28
  959.9 67.8 %collective-permute-done.28 = f32[2,256,512]{2,1,0:T(8,128)S(1)} collective-permute-done((f32[2,256,512]{2,1,0:T(8,128)S(1)}, f32[2,256,512]{2,1,0:T(8,128)S(1)}, u32[]{:S(2)}, u32[]{:S(2)}) %collective-permute-start.28) | collective-permute-done | bytes 1048608 | tf_op jit(solution)/shard_map/ppermute | solution.py:14
  1027.7 22.5 %collective-permute-done.29 = f32[2,256,512]{2,1,0:T(8,128)S(1)} collective-permute-done((f32[2,256,512]{2,1,0:T(8,128)S(1)}, f32[2,256,512]{2,1,0:T(8,128)S(1)}, u32[]{:S(2)}, u32[]{:S(2)}) %collective-permute-start.29) | collective-permute-done | bytes 1048608 | tf_op jit(solution)/shard_map/ppermute | solution.py:14
  1053.0 22.4 %collective-permute-done.30 = f32[2,256,512]{2,1,0:T(8,128)S(1)} collective-permute-done((f32[2,256,512]{2,1,0:T(8,128)S(1)}, f32[2,256,512]{2,1,0:T(8,128)S(1)}, u32[]{:S(2)}, u32[]{:S(2)}) %collective-permute-start.30) | collective-permute-done | bytes 1048608 | tf_op jit(solution)/shard_map/ppermute | solution.py:14
  1075.3 22.5 %collective-permute-done.31 = f32[2,256,512]{2,1,0:T(8,128)S(1)} collective-permute-done((f32[2,256,512]{2,1,0:T(8,128)S(1)}, f32[2,256,512]{2,1,0:T(8,128)S(1)}, u32[]{:S(2)}, u32[]{:S(2)}) %collective-permute-start.31) | collective-permute-done | bytes 1048608 | tf_op jit(solution)/shard_map/ppermute | solution.py:14
  1098.4 3.7 collective-permute-start.32
  1102.3 22.0 %collective-permute-done.32 = f32[2,256,512]{2,1,0:T(8,128)S(1)} collective-permute-done((f32[2,256,512]{2,1,0:T(8,128)S(1)}, f32[2,256,512]{2,1,0:T(8,128)S(1)}, u32[]{:S(2)}, u32[]{:S(2)}) %collective-permute-start.32) | collective-permute-done | bytes 1048608 | tf_op jit(solution)/shard_map/ppermute | solution.py:14
  1124.3 22.5 %collective-permute-done.33 = f32[2,256,512]{2,1,0:T(8,128)S(1)} collective-permute-done((f32[2,256,512]{2,1,0:T(8,128)S(1)}, f32[2,256,512]{2,1,0:T(8,128)S(1)}, u32[]{:S(2)}, u32[]{:S(2)}) %collective-permute-start.33) | collective-permute-done | bytes 1048608 | tf_op jit(solution)/shard_map/ppermute | solution.py:14
  1147.5 2.8 collective-permute-start.34
  1150.6 21.2 %collective-permute-done.34 = f32[2,256,512]{2,1,0:T(8,128)S(1)} collective-permute-done((f32[2,256,512]{2,1,0:T(8,128)S(1)}, f32[2,256,512]{2,1,0:T(8,128)S(1)}, u32[]{:S(2)}, u32[]{:S(2)}) %collective-permute-start.34) | collective-permute-done | bytes 1048608 | tf_op jit(solution)/shard_map/ppermute | solution.py:14
  1172.0 22.2 %collective-permute-done.35 = f32[2,256,512]{2,1,0:T(8,128)S(1)} collective-permute-done((f32[2,256,512]{2,1,0:T(8,128)S(1)}, f32[2,256,512]{2,1,0:T(8,128)S(1)}, u32[]{:S(2)}, u32[]{:S(2)}) %collective-permute-start.35) | collective-permute-done | bytes 1048608 | tf_op jit(solution)/shard_map/ppermute | solution.py:14
  1194.2 3.5 fusion.19
  1197.7 49.0 %reduce-scatter.2.cloned.1.call-done = f32[256,1024]{1,0:T(8,128)} async-done(((f32[256,4096]{1,0:T(8,128)}), f32[256,1024]{1,0:T(8,128)}) %reduce-scatter.2.cloned.1.call-update) | async-done | bytes 1048592 | tf_op jit(solution)/shard_map/reduce_scatter | solution.py:180
  (89 shorter events, 38.6 us)
Async XLA Ops:
  6.5 2.5 copy-start
  6.5 11.1 copy-start.3
  6.5 1240.2 %reduce-scatter.2.cloned.1.call-start = ((), (), s32[]{:S(2)}) async-start(), calls=%async_computation.1 | async-start | bytes 5242880 | tf_op jit(solution)/shard_map/reduce_scatter | solution.py:180
  14.0 25.7 %collective-permute-start.12 = (f32[2,256,512]{2,1,0:T(8,128)}, f32[2,256,512]{2,1,0:T(8,128)}, u32[]{:S(2)}, u32[]{:S(2)}) collective-permute-start(f32[2,256,512]{2,1,0:T(8,128)} %pad_maximum_fusion.1), channel_id=1, source_target_pairs={{0,128},{4,132},{8,136},{12,140},{16,144},{20,148},{24,152},{28,15... | collective-permute-start | bytes 3145736 | tf_op jit(solution)/shard_map/ppermute | solution.py:14
  18.8 43.5 %collective-permute-start = (f32[2,256,512]{2,1,0:T(8,128)}, f32[2,256,512]{2,1,0:T(8,128)}, u32[]{:S(2)}, u32[]{:S(2)}) collective-permute-start(f32[2,256,512]{2,1,0:T(8,128)} %pad_maximum_fusion), channel_id=1, source_target_pairs={{0,128},{4,132},{8,136},{12,140},{16,144},{20,148},{24,152},{28,15... | collective-permute-start | bytes 3145736 | tf_op jit(solution)/shard_map/ppermute | solution.py:14
  19.9 64.8 %collective-permute-start.1 = (f32[2,256,512]{2,1,0:T(8,128)}, f32[2,256,512]{2,1,0:T(8,128)}, u32[]{:S(2)}, u32[]{:S(2)}) collective-permute-start(f32[2,256,512]{2,1,0:T(8,128)} %stack.34), channel_id=1, source_target_pairs={{0,128},{4,132},{8,136},{12,140},{16,144},{20,148},{24,152},{28,15... | collective-permute-start | bytes 3145736 | tf_op jit(solution)/shard_map/ppermute | solution.py:14
  24.0 83.2 %collective-permute-start.13 = (f32[2,256,512]{2,1,0:T(8,128)}, f32[2,256,512]{2,1,0:T(8,128)}, u32[]{:S(2)}, u32[]{:S(2)}) collective-permute-start(f32[2,256,512]{2,1,0:T(8,128)} %stack.39), channel_id=1, source_target_pairs={{0,128},{4,132},{8,136},{12,140},{16,144},{20,148},{24,152},{28,15... | collective-permute-start | bytes 3145736 | tf_op jit(solution)/shard_map/ppermute | solution.py:14
  112.2 25.8 %collective-permute-start.14 = (f32[2,256,512]{2,1,0:T(8,128)}, f32[2,256,512]{2,1,0:T(8,128)S(1)}, u32[]{:S(2)}, u32[]{:S(2)}) collective-permute-start(f32[2,256,512]{2,1,0:T(8,128)} %get-tuple-element.38), channel_id=1, source_target_pairs={{0,64},{4,68},{8,72},{12,76},{16,80},{20,84},{24,88},{28,92},{32,9... | collective-permute-start | bytes 3145736 | tf_op jit(solution)/shard_map/ppermute | solution.py:14
  116.1 44.5 %collective-permute-start.15 = (f32[2,256,512]{2,1,0:T(8,128)}, f32[2,256,512]{2,1,0:T(8,128)S(1)}, u32[]{:S(2)}, u32[]{:S(2)}) collective-permute-start(f32[2,256,512]{2,1,0:T(8,128)} %get-tuple-element.37), channel_id=1, source_target_pairs={{0,64},{4,68},{8,72},{12,76},{16,80},{20,84},{24,88},{28,92},{32,9... | collective-permute-start | bytes 3145736 | tf_op jit(solution)/shard_map/ppermute | solution.py:14
  116.1 66.9 %collective-permute-start.2 = (f32[2,256,512]{2,1,0:T(8,128)}, f32[2,256,512]{2,1,0:T(8,128)S(1)}, u32[]{:S(2)}, u32[]{:S(2)}) collective-permute-start(f32[2,256,512]{2,1,0:T(8,128)} %get-tuple-element.59), channel_id=1, source_target_pairs={{0,64},{4,68},{8,72},{12,76},{16,80},{20,84},{24,88},{28,92},{32,9... | collective-permute-start | bytes 3145736 | tf_op jit(solution)/shard_map/ppermute | solution.py:14
  119.1 86.5 %collective-permute-start.3 = (f32[2,256,512]{2,1,0:T(8,128)}, f32[2,256,512]{2,1,0:T(8,128)}, u32[]{:S(2)}, u32[]{:S(2)}) collective-permute-start(f32[2,256,512]{2,1,0:T(8,128)} %get-tuple-element.60), channel_id=1, source_target_pairs={{0,64},{4,68},{8,72},{12,76},{16,80},{20,84},{24,88},{28,92},{32,9... | collective-permute-start | bytes 3145736 | tf_op jit(solution)/shard_map/ppermute | solution.py:14
  138.1 67.5 %copy-start.4 = (f32[2,256,512]{2,1,0:T(8,128)}, f32[2,256,512]{2,1,0:T(8,128)S(1)}, u32[]{:S(2)}) copy-start(f32[2,256,512]{2,1,0:T(8,128)S(1)} %collective-permute-done.14) | copy-start | bytes 3145732
  160.6 45.1 %copy-start.6 = (f32[2,256,512]{2,1,0:T(8,128)}, f32[2,256,512]{2,1,0:T(8,128)S(1)}, u32[]{:S(2)}) copy-start(f32[2,256,512]{2,1,0:T(8,128)S(1)} %collective-permute-done.15) | copy-start | bytes 3145732
  183.0 22.6 %copy-start.8 = (f32[2,256,512]{2,1,0:T(8,128)}, f32[2,256,512]{2,1,0:T(8,128)S(1)}, u32[]{:S(2)}) copy-start(f32[2,256,512]{2,1,0:T(8,128)S(1)} %collective-permute-done.2) | copy-start | bytes 3145732
  211.4 22.4 %collective-permute-start.16 = (f32[2,256,512]{2,1,0:T(8,128)S(1)}, f32[2,256,512]{2,1,0:T(8,128)}, u32[]{:S(2)}, u32[]{:S(2)}) collective-permute-start(f32[2,256,512]{2,1,0:T(8,128)S(1)} %get-tuple-element.24), channel_id=1, source_target_pairs={{0,32},{4,36},{8,40},{12,44},{16,48},{20,52},{24,56},{28,60},{32,0... | collective-permute-start | bytes 3145736 | tf_op jit(solution)/shard_map/ppermute | solution.py:14
  212.6 43.7 %collective-permute-start.17 = (f32[2,256,512]{2,1,0:T(8,128)S(1)}, f32[2,256,512]{2,1,0:T(8,128)}, u32[]{:S(2)}, u32[]{:S(2)}) collective-permute-start(f32[2,256,512]{2,1,0:T(8,128)S(1)} %get-tuple-element.23), channel_id=1, source_target_pairs={{0,32},{4,36},{8,40},{12,44},{16,48},{20,52},{24,56},{28,60},{32,0... | collective-permute-start | bytes 3145736 | tf_op jit(solution)/shard_map/ppermute | solution.py:14
  212.9 65.9 %collective-permute-start.4 = (f32[2,256,512]{2,1,0:T(8,128)S(1)}, f32[2,256,512]{2,1,0:T(8,128)}, u32[]{:S(2)}, u32[]{:S(2)}) collective-permute-start(f32[2,256,512]{2,1,0:T(8,128)S(1)} %get-tuple-element.57), channel_id=1, source_target_pairs={{0,32},{4,36},{8,40},{12,44},{16,48},{20,52},{24,56},{28,60},{32,0... | collective-permute-start | bytes 3145736 | tf_op jit(solution)/shard_map/ppermute | solution.py:14
  214.1 87.2 %collective-permute-start.5 = (f32[2,256,512]{2,1,0:T(8,128)}, f32[2,256,512]{2,1,0:T(8,128)}, u32[]{:S(2)}, u32[]{:S(2)}) collective-permute-start(f32[2,256,512]{2,1,0:T(8,128)} %get-tuple-element.58), channel_id=1, source_target_pairs={{0,32},{4,36},{8,40},{12,44},{16,48},{20,52},{24,56},{28,60},{32,0... | collective-permute-start | bytes 3145736 | tf_op jit(solution)/shard_map/ppermute | solution.py:14
  306.9 31.6 %collective-permute-start.18 = (f32[2,256,512]{2,1,0:T(8,128)}, f32[2,256,512]{2,1,0:T(8,128)S(1)}, u32[]{:S(2)}, u32[]{:S(2)}) collective-permute-start(f32[2,256,512]{2,1,0:T(8,128)} %get-tuple-element.22), channel_id=1, source_target_pairs={{0,16},{4,20},{8,24},{12,28},{16,0},{20,4},{24,8},{28,12},{32,48},... | collective-permute-start | bytes 3145736 | tf_op jit(solution)/shard_map/ppermute | solution.py:14
  313.6 57.1 %collective-permute-start.19 = (f32[2,256,512]{2,1,0:T(8,128)}, f32[2,256,512]{2,1,0:T(8,128)S(1)}, u32[]{:S(2)}, u32[]{:S(2)}) collective-permute-start(f32[2,256,512]{2,1,0:T(8,128)} %get-tuple-element.21), channel_id=1, source_target_pairs={{0,16},{4,20},{8,24},{12,28},{16,0},{20,4},{24,8},{28,12},{32,48},... | collective-permute-start | bytes 3145736 | tf_op jit(solution)/shard_map/ppermute | solution.py:14
  313.6 97.1 %collective-permute-start.6 = (f32[2,256,512]{2,1,0:T(8,128)}, f32[2,256,512]{2,1,0:T(8,128)S(1)}, u32[]{:S(2)}, u32[]{:S(2)}) collective-permute-start(f32[2,256,512]{2,1,0:T(8,128)} %get-tuple-element.55), channel_id=1, source_target_pairs={{0,16},{4,20},{8,24},{12,28},{16,0},{20,4},{24,8},{28,12},{32,48},... | collective-permute-start | bytes 3145736 | tf_op jit(solution)/shard_map/ppermute | solution.py:14
  319.0 141.8 %collective-permute-start.7 = (f32[2,256,512]{2,1,0:T(8,128)}, f32[2,256,512]{2,1,0:T(8,128)}, u32[]{:S(2)}, u32[]{:S(2)}) collective-permute-start(f32[2,256,512]{2,1,0:T(8,128)} %get-tuple-element.56), channel_id=1, source_target_pairs={{0,16},{4,20},{8,24},{12,28},{16,0},{20,4},{24,8},{28,12},{32,48},... | collective-permute-start | bytes 3145736 | tf_op jit(solution)/shard_map/ppermute | solution.py:14
  338.5 122.2 %copy-start.5 = (f32[2,256,512]{2,1,0:T(8,128)}, f32[2,256,512]{2,1,0:T(8,128)S(1)}, u32[]{:S(2)}) copy-start(f32[2,256,512]{2,1,0:T(8,128)S(1)} %collective-permute-done.18) | copy-start | bytes 3145732
  370.6 90.1 %copy-start.7 = (f32[2,256,512]{2,1,0:T(8,128)}, f32[2,256,512]{2,1,0:T(8,128)S(1)}, u32[]{:S(2)}) copy-start(f32[2,256,512]{2,1,0:T(8,128)S(1)} %collective-permute-done.19) | copy-start | bytes 3145732
  410.7 50.0 %copy-start.9 = (f32[2,256,512]{2,1,0:T(8,128)}, f32[2,256,512]{2,1,0:T(8,128)S(1)}, u32[]{:S(2)}) copy-start(f32[2,256,512]{2,1,0:T(8,128)S(1)} %collective-permute-done.6) | copy-start | bytes 3145732
  466.5 148.5 %collective-permute-start.20 = (f32[2,256,512]{2,1,0:T(8,128)S(1)}, f32[2,256,512]{2,1,0:T(8,128)}, u32[]{:S(2)}, u32[]{:S(2)}) collective-permute-start(f32[2,256,512]{2,1,0:T(8,128)S(1)} %get-tuple-element.20), channel_id=1, source_target_pairs={{0,8},{4,12},{8,0},{12,4},{16,24},{20,28},{24,16},{28,20},{32,40},... | collective-permute-start | bytes 3145736 | tf_op jit(solution)/shard_map/ppermute | solution.py:14
  501.9 135.6 %collective-permute-start.21 = (f32[2,256,512]{2,1,0:T(8,128)S(1)}, f32[2,256,512]{2,1,0:T(8,128)}, u32[]{:S(2)}, u32[]{:S(2)}) collective-permute-start(f32[2,256,512]{2,1,0:T(8,128)S(1)} %get-tuple-element.19), channel_id=1, source_target_pairs={{0,8},{4,12},{8,0},{12,4},{16,24},{20,28},{24,16},{28,20},{32,40},... | collective-permute-start | bytes 3145736 | tf_op jit(solution)/shard_map/ppermute | solution.py:14
  501.9 158.1 %collective-permute-start.8 = (f32[2,256,512]{2,1,0:T(8,128)S(1)}, f32[2,256,512]{2,1,0:T(8,128)}, u32[]{:S(2)}, u32[]{:S(2)}) collective-permute-start(f32[2,256,512]{2,1,0:T(8,128)S(1)} %get-tuple-element.53), channel_id=1, source_target_pairs={{0,8},{4,12},{8,0},{12,4},{16,24},{20,28},{24,16},{28,20},{32,40},... | collective-permute-start | bytes 3145736 | tf_op jit(solution)/shard_map/ppermute | solution.py:14
  504.2 178.2 %collective-permute-start.9 = (f32[2,256,512]{2,1,0:T(8,128)}, f32[2,256,512]{2,1,0:T(8,128)}, u32[]{:S(2)}, u32[]{:S(2)}) collective-permute-start(f32[2,256,512]{2,1,0:T(8,128)} %get-tuple-element.54), channel_id=1, source_target_pairs={{0,8},{4,12},{8,0},{12,4},{16,24},{20,28},{24,16},{28,20},{32,40},... | collective-permute-start | bytes 3145736 | tf_op jit(solution)/shard_map/ppermute | solution.py:14
  688.0 23.9 %collective-permute-start.10 = (f32[2,256,512]{2,1,0:T(8,128)}, f32[2,256,512]{2,1,0:T(8,128)S(1)}, u32[]{:S(2)}, u32[]{:S(2)}) collective-permute-start(f32[2,256,512]{2,1,0:T(8,128)} %get-tuple-element.51), channel_id=1, source_target_pairs={{0,4},{4,0},{8,12},{12,8},{16,20},{20,16},{24,28},{28,24},{32,36},... | collective-permute-start | bytes 3145736 | tf_op jit(solution)/shard_map/ppermute | solution.py:14
  688.0 46.4 %collective-permute-start.11 = (f32[2,256,512]{2,1,0:T(8,128)}, f32[2,256,512]{2,1,0:T(8,128)S(1)}, u32[]{:S(2)}, u32[]{:S(2)}) collective-permute-start(f32[2,256,512]{2,1,0:T(8,128)} %get-tuple-element.52), channel_id=1, source_target_pairs={{0,4},{4,0},{8,12},{12,8},{16,20},{20,16},{24,28},{28,24},{32,36},... | collective-permute-start | bytes 3145736 | tf_op jit(solution)/shard_map/ppermute | solution.py:14
  689.5 67.4 %collective-permute-start.22 = (f32[2,256,512]{2,1,0:T(8,128)}, f32[2,256,512]{2,1,0:T(8,128)S(1)}, u32[]{:S(2)}, u32[]{:S(2)}) collective-permute-start(f32[2,256,512]{2,1,0:T(8,128)} %get-tuple-element.18), channel_id=1, source_target_pairs={{0,4},{4,0},{8,12},{12,8},{16,20},{20,16},{24,28},{28,24},{32,36},... | collective-permute-start | bytes 3145736 | tf_op jit(solution)/shard_map/ppermute | solution.py:14
  689.6 89.9 %collective-permute-start.23 = (f32[2,256,512]{2,1,0:T(8,128)}, f32[2,256,512]{2,1,0:T(8,128)}, u32[]{:S(2)}, u32[]{:S(2)}) collective-permute-start(f32[2,256,512]{2,1,0:T(8,128)} %get-tuple-element.17), channel_id=1, source_target_pairs={{0,4},{4,0},{8,12},{12,8},{16,20},{20,16},{24,28},{28,24},{32,36},... | collective-permute-start | bytes 3145736 | tf_op jit(solution)/shard_map/ppermute | solution.py:14
  814.0 22.9 %collective-permute-start.24 = (f32[2,256,512]{2,1,0:T(8,128)S(1)}, f32[2,256,512]{2,1,0:T(8,128)S(1)}, u32[]{:S(2)}, u32[]{:S(2)}) collective-permute-start(f32[2,256,512]{2,1,0:T(8,128)S(1)} %get-tuple-element.42), channel_id=1, source_target_pairs={{0,4},{4,0},{8,12},{12,8},{16,20},{20,16},{24,28},{28,24},{32,36},... | collective-permute-start | bytes 3145736 | tf_op jit(solution)/shard_map/ppermute | solution.py:14
  814.2 45.2 %collective-permute-start.25 = (f32[2,256,512]{2,1,0:T(8,128)S(1)}, f32[2,256,512]{2,1,0:T(8,128)S(1)}, u32[]{:S(2)}, u32[]{:S(2)}) collective-permute-start(f32[2,256,512]{2,1,0:T(8,128)S(1)} %get-tuple-element.41), channel_id=1, source_target_pairs={{0,4},{4,0},{8,12},{12,8},{16,20},{20,16},{24,28},{28,24},{32,36},... | collective-permute-start | bytes 3145736 | tf_op jit(solution)/shard_map/ppermute | solution.py:14
  860.0 71.0 %collective-permute-start.26 = (f32[2,256,512]{2,1,0:T(8,128)S(1)}, f32[2,256,512]{2,1,0:T(8,128)S(1)}, u32[]{:S(2)}, u32[]{:S(2)}) collective-permute-start(f32[2,256,512]{2,1,0:T(8,128)S(1)} %get-tuple-element.14), channel_id=1, source_target_pairs={{0,8},{4,12},{8,0},{12,4},{16,24},{20,28},{24,16},{28,20},{32,40},... | collective-permute-start | bytes 3145736 | tf_op jit(solution)/shard_map/ppermute | solution.py:14
  861.9 91.5 %collective-permute-start.27 = (f32[2,256,512]{2,1,0:T(8,128)S(1)}, f32[2,256,512]{2,1,0:T(8,128)S(1)}, u32[]{:S(2)}, u32[]{:S(2)}) collective-permute-start(f32[2,256,512]{2,1,0:T(8,128)S(1)} %get-tuple-element.13), channel_id=1, source_target_pairs={{0,8},{4,12},{8,0},{12,4},{16,24},{20,28},{24,16},{28,20},{32,40},... | collective-permute-start | bytes 3145736 | tf_op jit(solution)/shard_map/ppermute | solution.py:14
  954.1 73.6 %collective-permute-start.28 = (f32[2,256,512]{2,1,0:T(8,128)S(1)}, f32[2,256,512]{2,1,0:T(8,128)S(1)}, u32[]{:S(2)}, u32[]{:S(2)}) collective-permute-start(f32[2,256,512]{2,1,0:T(8,128)S(1)} %get-tuple-element.12), channel_id=1, source_target_pairs={{0,16},{4,20},{8,24},{12,28},{16,0},{20,4},{24,8},{28,12},{32,48},... | collective-permute-start | bytes 3145736 | tf_op jit(solution)/shard_map/ppermute | solution.py:14
  957.9 92.2 %collective-permute-start.29 = (f32[2,256,512]{2,1,0:T(8,128)S(1)}, f32[2,256,512]{2,1,0:T(8,128)S(1)}, u32[]{:S(2)}, u32[]{:S(2)}) collective-permute-start(f32[2,256,512]{2,1,0:T(8,128)S(1)} %get-tuple-element.11), channel_id=1, source_target_pairs={{0,16},{4,20},{8,24},{12,28},{16,0},{20,4},{24,8},{28,12},{32,48},... | collective-permute-start | bytes 3145736 | tf_op jit(solution)/shard_map/ppermute | solution.py:14
  1050.8 24.5 %collective-permute-start.30 = (f32[2,256,512]{2,1,0:T(8,128)S(1)}, f32[2,256,512]{2,1,0:T(8,128)S(1)}, u32[]{:S(2)}, u32[]{:S(2)}) collective-permute-start(f32[2,256,512]{2,1,0:T(8,128)S(1)} %get-tuple-element.10), channel_id=1, source_target_pairs={{0,32},{4,36},{8,40},{12,44},{16,48},{20,52},{24,56},{28,60},{32,0... | collective-permute-start | bytes 3145736 | tf_op jit(solution)/shard_map/ppermute | solution.py:14
  1052.8 45.0 %collective-permute-start.31 = (f32[2,256,512]{2,1,0:T(8,128)S(1)}, f32[2,256,512]{2,1,0:T(8,128)S(1)}, u32[]{:S(2)}, u32[]{:S(2)}) collective-permute-start(f32[2,256,512]{2,1,0:T(8,128)S(1)} %get-tuple-element.9), channel_id=1, source_target_pairs={{0,32},{4,36},{8,40},{12,44},{16,48},{20,52},{24,56},{28,60},{32,0... | collective-permute-start | bytes 3145736 | tf_op jit(solution)/shard_map/ppermute | solution.py:14
  1098.4 25.9 %collective-permute-start.32 = (f32[2,256,512]{2,1,0:T(8,128)S(1)}, f32[2,256,512]{2,1,0:T(8,128)S(1)}, u32[]{:S(2)}, u32[]{:S(2)}) collective-permute-start(f32[2,256,512]{2,1,0:T(8,128)S(1)} %get-tuple-element.8), channel_id=1, source_target_pairs={{0,64},{4,68},{8,72},{12,76},{16,80},{20,84},{24,88},{28,92},{32,9... | collective-permute-start | bytes 3145736 | tf_op jit(solution)/shard_map/ppermute | solution.py:14
  1102.2 44.6 %collective-permute-start.33 = (f32[2,256,512]{2,1,0:T(8,128)S(1)}, f32[2,256,512]{2,1,0:T(8,128)S(1)}, u32[]{:S(2)}, u32[]{:S(2)}) collective-permute-start(f32[2,256,512]{2,1,0:T(8,128)S(1)} %get-tuple-element.7), channel_id=1, source_target_pairs={{0,64},{4,68},{8,72},{12,76},{16,80},{20,84},{24,88},{28,92},{32,9... | collective-permute-start | bytes 3145736 | tf_op jit(solution)/shard_map/ppermute | solution.py:14
  1146.8 47.4 %copy-start.2 = (bf16[512,4096]{1,0:T(8,128)(2,1)S(1)}, bf16[512,4096]{1,0:T(8,128)(2,1)}, u32[]{:S(2)}) copy-start(bf16[512,4096]{1,0:T(8,128)(2,1)} %param.21) | copy-start | bytes 12582916
  1146.8 47.4 %copy-start.10 = (bf16[256,512]{1,0:T(8,128)(2,1)S(1)}, bf16[256,512]{1,0:T(8,128)(2,1)}, u32[]{:S(2)}) copy-start(bf16[256,512]{1,0:T(8,128)(2,1)} %param.12) | copy-start | bytes 786436
  1146.8 47.4 %copy-start.11 = (f32[512]{0:T(512)S(1)}, f32[512]{0:T(512)}, u32[]{:S(2)}) copy-start(f32[512]{0:T(512)} %param.13) | copy-start | bytes 6148
  1147.5 24.3 %collective-permute-start.34 = (f32[2,256,512]{2,1,0:T(8,128)S(1)}, f32[2,256,512]{2,1,0:T(8,128)S(1)}, u32[]{:S(2)}, u32[]{:S(2)}) collective-permute-start(f32[2,256,512]{2,1,0:T(8,128)S(1)} %get-tuple-element.6), channel_id=1, source_target_pairs={{0,128},{4,132},{8,136},{12,140},{16,144},{20,148},{24,152},{28,15... | collective-permute-start | bytes 3145736 | tf_op jit(solution)/shard_map/ppermute | solution.py:14
  1150.3 43.9 %collective-permute-start.35 = (f32[2,256,512]{2,1,0:T(8,128)S(1)}, f32[2,256,512]{2,1,0:T(8,128)S(1)}, u32[]{:S(2)}, u32[]{:S(2)}) collective-permute-start(f32[2,256,512]{2,1,0:T(8,128)S(1)} %get-tuple-element.5), channel_id=1, source_target_pairs={{0,128},{4,132},{8,136},{12,140},{16,144},{20,148},{24,152},{28,15... | collective-permute-start | bytes 3145736 | tf_op jit(solution)/shard_map/ppermute | solution.py:14
  1194.2 54.6 %copy-start.1 = (f32[64,64]{1,0:T(8,128)S(1)}, f32[64,64]{1,0:T(8,128)}, u32[]{:S(2)}) copy-start(f32[64,64]{1,0:T(8,128)} %param.17) | copy-start | bytes 49156
Sparse Core Ops, SparseCore 0:
  1197.9 48.8 reduce-scatter.1
where the time goes:
time: 1260 us
  waiting for transfers between devices  1070 us (85%)
  starting transfers between devices  88.4 us (7%)
  other arithmetic  42 us (3%)
  matrix products  38.6 us (3%)
  between operations  14.1 us (1%)
    ppermute x36, waiting for transfers between devices, from_partner(): return lax.ppermute(value, axis, pairs)  1020 us
    ppermute x36, starting transfers between devices, from_partner(): return lax.ppermute(value, axis, pairs)  88.4 us
    reduce_scatter x1, waiting for transfers between devices, shards(): lax.psum_scatter(partial_out, 'ch', scatter_dimension=1, tiled=True)  49 us
    select_n x6, other arithmetic, forward_bits(): imag_part = jnp.where(upper_half, diff_imag, imag_part + recv_imag)  31.6 us
  transfers between devices with their start and end apart: 37, of which 37 were waited for; matrix products, arithmetic and copies ran while one was open for 0% of the time, Pallas kernels for 0%

commit v1 on v0

v1 whole, which is shorter than its diff:
```python
import math

import jax
import jax.numpy as jnp
from jax import lax
from jax.experimental import pallas as pl
from jax.experimental.pallas import tpu as pltpu
from jax.sharding import PartitionSpec as P

F32 = jnp.float32
BF16 = jnp.bfloat16
MESH = pl.DeviceIdType.MESH

SEQ_LEN = 16384
DEVS = 64
ROWS = 256
CHANS = 512
OWN = 8
HID = 64
PARTS = 4
QUARTER = SEQ_LEN // PARTS
STEP = 256
TAP = 64
DEPTH = 1024
TOP = SEQ_LEN - TAP
COLS = 1024
INV_TURN = 1.0 / (2.0 * math.pi)
COS_POLY = (6.283185159611168, -41.34165492934356, 81.60099819261757, -76.54965682073457, 39.53581371237487)


def turn_cos(turns):
    near = turns - jnp.round(turns)
    arg = 0.25 - jnp.abs(near)
    square = arg * arg
    c0, c1, c2, c3, c4 = COS_POLY
    return arg * (c0 + square * (c1 + square * (c2 + square * (c3 + square * c4))))


def split_two(value):
    high = value.astype(BF16)
    return high, (value - high.astype(F32)).astype(BF16)


def dot(left, right):
    return jnp.dot(left, right, preferred_element_type=F32)


def dot_nt(left, right):
    return lax.dot_general(left, right, (((1,), (1,)), ((), ())), preferred_element_type=F32)


def tile_lanes(value):
    return jnp.concatenate([value] * PARTS, axis=1)


def iota(shape, axis):
    return lax.broadcasted_iota(jnp.int32, shape, axis)


def filter_weights(own_first, decay_ref, w1_ref, b1_ref, w2_ref, b2_ref, hi_ref, fix_ref,
                   first_ref, second_ref, bias_ref, third_ref, env_ref):
    wide = PARTS * HID
    part = iota((16, wide), 1) >> 6
    freq = (iota((16, wide), 0) + 1).astype(F32)
    turns = freq * (TOP - QUARTER * part).astype(F32) * (1.0 / SEQ_LEN)
    cos_top, sin_top = turn_cos(turns), turn_cos(turns - 0.25)
    w_lin = tile_lanes(w1_ref[0:1, :]) * INV_TURN
    w_cos = tile_lanes(w1_ref[1:17, :]) * INV_TURN
    w_sin = tile_lanes(w1_ref[17:33, :]) * INV_TURN
    main = jnp.concatenate(
        [w_cos * cos_top + w_sin * sin_top, w_cos * sin_top - w_sin * cos_top], axis=0
    )
    main_hi = main.astype(BF16).astype(F32)
    main_lo = main - main_hi
    part_row = iota((1, wide), 1) >> 6
    top_row = (TOP - QUARTER * part_row).astype(F32) * (1.0 / SEQ_LEN)
    slope = -w_lin / PARTS
    const = w_lin * top_row + tile_lanes(b1_ref[...]) * INV_TURN - 0.25
    wrap = jnp.where(part_row == PARTS - 1, w_lin, 0.0)
    extra = jnp.zeros((32, wide), F32)
    row = iota((32, wide), 0)
    place = 0
    for value, pieces, repeat in ((slope, 2, 2), (const, 3, 1), (wrap, 3, 1)):
        rest = value
        for _ in range(pieces):
            piece = rest.astype(BF16).astype(F32)
            rest = rest - piece
            for _ in range(repeat):
                extra = jnp.where(row == place, piece, extra)
                place += 1
    first_ref[...] = jnp.concatenate([main_hi, main_hi, main_lo, extra], axis=0).astype(BF16)

    own_block = iota((wide, wide), 0) >> 6 == iota((wide, wide), 1) >> 6
    w2_rows = jnp.concatenate([w2_ref[...] * INV_TURN] * PARTS, axis=0)
    w2_full = jnp.where(own_block, tile_lanes(w2_rows), 0.0)
    w2_hi, w2_lo = split_two(w2_full)
    second_ref[0] = w2_hi
    second_ref[1] = w2_lo
    bias_ref[...] = tile_lanes(b2_ref[...]) * INV_TURN - 0.25

    lhs_rows = PARTS * OWN
    pick = iota((lhs_rows, CHANS), 1) == own_first + (iota((lhs_rows, CHANS), 0) & (OWN - 1))
    chosen = jnp.where(pick, 1.0, 0.0).astype(BF16)
    keep = iota((lhs_rows, wide), 1) >> 6 == iota((lhs_rows, wide), 0) >> 3
    hi_part = jnp.concatenate([hi_ref[...]] * PARTS, axis=0)
    fix_part = jnp.concatenate([(fix_ref[...].astype(F32) * 2.0 ** (-11)).astype(BF16)] * PARTS, axis=0)
    third_ref[...] = jnp.concatenate(
        [jnp.where(keep, dot_nt(chosen, hi_part), 0.0), jnp.where(keep, dot_nt(chosen, fix_part), 0.0)], axis=0
    ).astype(BF16)
    env_ref[...] = jnp.broadcast_to(
        jnp.sum(jnp.where(pick, decay_ref[...], 0.0), axis=1, keepdims=True), (lhs_rows, 128)
    )


def filter_step(step, first_ref, second_ref, bias_ref, third_ref, env_ref, filt_ref):
    lane = iota((STEP, 128), 1)
    where_in = (iota((STEP, 128), 0) + step * STEP).astype(F32)
    freq = ((lane & 15) + 1).astype(F32)
    shift = jnp.where((lane & 16) == 0, 0.0, 0.25)
    value = turn_cos(where_in * freq * (1.0 / SEQ_LEN) - shift)
    value = jnp.where(lane < 96, value, where_in * (1.0 / QUARTER))
    value = jnp.where(lane < 100, value, 1.0)
    value = jnp.where(lane < 103, value, jnp.where(where_in > TOP - QUARTER * (PARTS - 1), 1.0, 0.0))
    value = jnp.where(lane < 106, value, 0.0)
    low = ((lane >= 32) & (lane < 64)) | (lane == 97) | (lane == 99)
    high = value.astype(BF16).astype(F32)
    feats = jnp.where(low, value - high, high).astype(BF16)
    one_hi, one_lo = split_two(turn_cos(dot(feats, first_ref[...])))
    turns = dot(one_hi, second_ref[0]) + dot(one_lo, second_ref[0]) + dot(one_hi, second_ref[1])
    two_hi, two_lo = split_two(turn_cos(turns + bias_ref[...]))
    both = dot_nt(third_ref[...], two_hi) + dot_nt(third_ref[...], two_lo)
    lhs_rows = PARTS * OWN
    shape = (lhs_rows, STEP)
    time = TOP - QUARTER * ((iota(shape, 0) >> 3)) - (iota(shape, 1) + step * STEP)
    time = jnp.where(time < 0, time + SEQ_LEN, time).astype(F32)
    rate = jnp.concatenate([env_ref[...]] * (STEP // 128), axis=1)
    envelope = jnp.exp(-rate * time) * jnp.sqrt(2.0 * rate + 1.0 / SEQ_LEN)
    filters = (both[:lhs_rows] + both[lhs_rows:]) * envelope
    for tile in range(STEP // 128):
        filt_ref[step * (STEP // 128) + tile] = filters[:, 128 * tile:128 * (tile + 1)]


def toeplitz_tiles(chan, filt_ref, toep_ref):
    shape = (TAP, 128)
    ahead = iota(shape, 1) >= iota(shape, 0)
    inside = iota(shape, 1) <= iota(shape, 0) + TAP

    def slanted(tile):
        row = lax.div(tile, QUARTER // 128) * OWN + chan
        taps = filt_ref[lax.rem(tile, QUARTER // 128), pl.ds(row, 1), :]
        return pltpu.roll(jnp.broadcast_to(taps, shape), 0, 1, stride=1, stride_axis=0)

    def block(index, before):
        for sub in range(DEPTH // 128):
            now = slanted(index * (DEPTH // 128) + sub)
            tile = jnp.where(ahead, now, before)
            if sub == DEPTH // 128 - 1:
                tile = jnp.where(inside | (index < SEQ_LEN // DEPTH - 1), tile, 0.0)
            toep_ref[chan, pl.ds(pl.multiple_of(index * TAP, TAP), TAP), sub * 128:(sub + 1) * 128] = tile.astype(BF16)
            before = now
        return before

    lax.fori_loop(0, SEQ_LEN // DEPTH, block, slanted(jnp.int32(SEQ_LEN // 128 - 1)))


def shifted(value, count):
    if count == 0:
        return value
    lane = iota(value.shape, 1) & 63
    return jnp.where(lane >= count, pltpu.roll(value, count, 1), 0.0)


def signal_columns(chan, recv_ref, cols_ref):
    first_half = iota((64, 128), 1) < 64

    def pair(tile):
        return jnp.concatenate([tile, pltpu.roll(tile, 64, 1)], axis=0).T

    low, high = (pair(recv_ref[half, pl.ds(chan, DEVS, stride=OWN), :]) for half in range(2))
    t01, t10, t23, t32 = low[:64], low[64:], high[:64], high[64:]
    t12 = jnp.where(first_half, t10, t32)
    t30 = jnp.where(first_half, shifted(t32, 1), t10)
    for back in range(DEPTH // 64):
        whole, rem = back // 4, back % 4
        if rem == 0:
            left, right = shifted(t01, whole), shifted(t23, whole)
        elif rem == 1:
            left, right = shifted(t30, whole), shifted(t12, whole)
        elif rem == 2:
            left, right = shifted(t23, whole + 1), shifted(t01, whole)
        else:
            left, right = shifted(t12, whole + 1), shifted(t30, whole)
        rows = slice(64 * (15 - back), 64 * (16 - back))
        cols_ref[rows, 0:128] = left.astype(BF16)
        cols_ref[rows, 128:256] = right.astype(BF16)


def convolve(chan, toep_ref, cols_ref, send_ref):
    left = jnp.zeros((64, 128), F32)
    right = jnp.zeros((64, 128), F32)
    for quad in range(4):
        part = dot(toep_ref[chan, 256 * quad:256 * (quad + 1), :], cols_ref[...])
        for sub in range(4):
            left = shifted(left, 4) + part[64 * sub:64 * (sub + 1), 0:128]
            right = shifted(right, 4) + part[64 * sub:64 * (sub + 1), 128:256]
    for half, value in enumerate((left, right)):
        turned = jnp.concatenate([value, pltpu.roll(value, 64, 1)], axis=0).T
        send_ref[half, pl.ds(chan, DEVS, stride=OWN), :] = turned[:64]


def block_kernel(sig_ref, gate_ref, skip_ref, decay_ref, w1_ref, b1_ref, w2_ref, b2_ref, hi_ref, fix_ref, wout_ref,
                 out_ref,
                 first_ref, second_ref, bias_ref, third_ref, env_ref, filt_ref, toep_ref, cols_ref,
                 sig_t, gate_t, recv_x, send_y, recv_y, gated_ref, wide_ref,
                 core_send, core_recv, far_send, far_recv,
                 wide_sem, x_send_sem, x_recv_sem, y_send_sem, y_recv_sem,
                 core_send_sem, core_recv_sem, far_send_sem, far_recv_sem):
    me = lax.axis_index("seq")
    group = lax.axis_index("ch")
    core = lax.rem(group, 2)
    chip = lax.div(group, 2)
    core_mate = chip * 2 + 1 - core
    far_mate = (1 - chip) * 2 + core

    barrier = pltpu.get_barrier_semaphore()

    @pl.loop(1, DEVS)
    def _(step):
        pl.semaphore_signal(barrier, inc=1, device_id={"seq": lax.rem(me + step, DEVS)}, device_id_type=MESH)

    for mate in (core_mate, far_mate):
        pl.semaphore_signal(barrier, inc=1, device_id={"ch": mate}, device_id_type=MESH)

    blocks = ((1 - chip) * 2 + 1 - core, far_mate, core_mate, group)
    loads = [
        pltpu.make_async_copy(
            wout_ref.at[:, pl.ds(pl.multiple_of(block * COLS, COLS), COLS)], wide_ref.at[slot], wide_sem.at[slot]
        )
        for slot, block in enumerate(blocks)
    ]
    for load in loads:
        load.start()

    for half in range(2):
        part = sig_ref[128 * half:128 * (half + 1), :].astype(F32)
        sig_t[half] = part.T
    own_rows = pl.ds(pl.multiple_of(me * OWN, OWN), OWN)
    recv_x[:, own_rows, :] = sig_t[:, own_rows, :]
    pl.semaphore_wait(barrier, DEVS + 1)

    @pl.loop(1, DEVS)
    def _(step):
        peer = lax.rem(me + step, DEVS)
        pltpu.make_async_remote_copy(
            src_ref=sig_t.at[:, pl.ds(pl.multiple_of(peer * OWN, OWN), OWN), :],
            dst_ref=recv_x.at[:, own_rows, :],
            send_sem=x_send_sem,
            recv_sem=x_recv_sem,
            device_id={"seq": peer},
            device_id_type=MESH,
        ).start()

    for half in range(2):
        gate_t[half] = gate_ref[128 * half:128 * (half + 1), :].astype(F32).T
    skip = jnp.broadcast_to(skip_ref[...], (128, CHANS)).T

    filter_weights(me * OWN, decay_ref, w1_ref, b1_ref, w2_ref, b2_ref, hi_ref, fix_ref,
                   first_ref, second_ref, bias_ref, third_ref, env_ref)

    @pl.loop(0, QUARTER // STEP)
    def _(step):
        filter_step(step, first_ref, second_ref, bias_ref, third_ref, env_ref, filt_ref)

    @pl.loop(0, OWN)
    def _(chan):
        toeplitz_tiles(chan, filt_ref, toep_ref)

    many = pl.ds(0, (DEVS - 1) * OWN)
    pltpu.make_async_copy(recv_x.at[:, many, :], recv_x.at[:, many, :], x_recv_sem).wait()

    @pl.loop(0, OWN)
    def _(chan):
        signal_columns(chan, recv_x, cols_ref)
        convolve(chan, toep_ref, cols_ref, send_y)

    for half in range(2):
        recv_y[half, own_rows, :] = send_y[half, own_rows, :]

        @pl.loop(1, DEVS)
        def _(step):
            peer = lax.rem(me + step, DEVS)
            pltpu.make_async_remote_copy(
                src_ref=send_y.at[half, pl.ds(pl.multiple_of(peer * OWN, OWN), OWN), :],
                dst_ref=recv_y.at[half, own_rows, :],
                send_sem=y_send_sem.at[half],
                recv_sem=y_recv_sem.at[half],
                device_id={"seq": peer},
                device_id_type=MESH,
            ).start()

    def to_core(half, which):
        return pltpu.make_async_remote_copy(
            src_ref=core_send.at[half, which], dst_ref=core_recv.at[half, which],
            send_sem=core_send_sem.at[half, which], recv_sem=core_recv_sem.at[half, which],
            device_id={"ch": core_mate}, device_id_type=MESH,
        )

    def to_far(half):
        return pltpu.make_async_remote_copy(
            src_ref=far_send.at[half], dst_ref=far_recv.at[half],
            send_sem=far_send_sem.at[half], recv_sem=far_recv_sem.at[half],
            device_id={"ch": far_mate}, device_id_type=MESH,
        )

    for load in loads:
        load.wait()
    for half in range(2):
        pltpu.make_async_copy(recv_y.at[half, many, :], recv_y.at[half, many, :], y_recv_sem.at[half]).wait()
        gated = gate_t[half] * (recv_y[half] + skip * sig_t[half])
        gated_ref[...] = gated.T.astype(BF16)
        core_send[half, 0] = dot(gated_ref[...], wide_ref[0])
        to_core(half, 0).start()
        far_send[half] = dot(gated_ref[...], wide_ref[1])
        to_core(half, 0).wait_recv()
        far_send[half] += core_recv[half, 0]
        to_far(half).start()
        core_send[half, 1] = dot(gated_ref[...], wide_ref[2])
        to_core(half, 1).start()
        total = dot(gated_ref[...], wide_ref[3])
        to_core(half, 1).wait_recv()
        core_recv[half, 1] += total
    for half in range(2):
        to_far(half).wait_recv()
        out_ref[128 * half:128 * (half + 1), :] = (core_recv[half, 1] + far_recv[half]).astype(BF16)

    pltpu.make_async_copy(sig_t.at[:, many, :], sig_t.at[:, many, :], x_send_sem).wait()
    for half in range(2):
        pltpu.make_async_copy(send_y.at[half, many, :], send_y.at[half, many, :], y_send_sem.at[half]).wait()
        for which in range(2):
            to_core(half, which).wait_send()
        to_far(half).wait_send()


def shards(signal, gate_in, skip_gain, decay, pos_weight1, pos_bias1, pos_weight2, pos_bias2, filt_hi, filt_fix,
           out_weight):
    vmem = pl.BlockSpec(memory_space=pltpu.VMEM)
    wide = PARTS * HID
    return pl.pallas_call(
        block_kernel,
        out_shape=jax.ShapeDtypeStruct((ROWS, COLS), BF16),
        in_specs=[vmem] * 10 + [pl.BlockSpec(memory_space=pl.ANY)],
        out_specs=vmem,
        scratch_shapes=[
            pltpu.VMEM((128, wide), BF16),
            pltpu.VMEM((2, wide, wide), BF16),
            pltpu.VMEM((1, wide), F32),
            pltpu.VMEM((2 * PARTS * OWN, wide), BF16),
            pltpu.VMEM((PARTS * OWN, 128), F32),
            pltpu.VMEM((QUARTER // 128, PARTS * OWN, 128), F32),
            pltpu.VMEM((OWN, SEQ_LEN // DEPTH * TAP, DEPTH), BF16),
            pltpu.VMEM((DEPTH, 256), BF16),
            pltpu.VMEM((2, CHANS, 128), F32),
            pltpu.VMEM((2, CHANS, 128), F32),
            pltpu.VMEM((2, CHANS, 128), F32),
            pltpu.VMEM((2, CHANS, 128), F32),
            pltpu.VMEM((2, CHANS, 128), F32),
            pltpu.VMEM((128, CHANS), BF16),
            pltpu.VMEM((4, CHANS, COLS), BF16),
            pltpu.VMEM((2, 2, 128, COLS), F32),
            pltpu.VMEM((2, 2, 128, COLS), F32),
            pltpu.VMEM((2, 128, COLS), F32),
            pltpu.VMEM((2, 128, COLS), F32),
            pltpu.SemaphoreType.DMA((4,)),
            pltpu.SemaphoreType.DMA,
            pltpu.SemaphoreType.DMA,
            pltpu.SemaphoreType.DMA((2,)),
            pltpu.SemaphoreType.DMA((2,)),
            pltpu.SemaphoreType.DMA((2, 2)),
            pltpu.SemaphoreType.DMA((2, 2)),
            pltpu.SemaphoreType.DMA((2,)),
            pltpu.SemaphoreType.DMA((2,)),
        ],
        compiler_params=pltpu.CompilerParams(
            collective_id=0, has_side_effects=True, vmem_limit_bytes=56 * 2**20
        ),
        name="hyena_block",
    )(
        signal, gate_in, skip_gain[None, :], decay[None, :], pos_weight1, pos_bias1[None, :], pos_weight2,
        pos_bias2[None, :], filt_hi, filt_fix, out_weight,
    )


def solution(mesh):
    return jax.shard_map(
        shards,
        mesh=mesh,
        in_specs=(
            P("seq", "ch"), P("seq", "ch"), P("ch"), P("ch"), P(), P(), P(), P(), P(None, "ch"), P(None, "ch"),
            P("ch", None),
        ),
        out_specs=P("seq", "ch"),
        check_vma=False,
    )
```

time: 1260 us -> 97.4 us (0.08)
  waiting for transfers between devices: 1070 us -> 0 us
  Pallas kernels: 0 us -> 95.4 us
  starting transfers between devices: 88.4 us -> 0 us
  other arithmetic: 42 us -> 0 us
  matrix products: 38.6 us -> 0 us
  between operations: 14.1 us -> 0.01 us
    ppermute x36 -> x0, waiting for transfers between devices: 1020 us -> none  [from_partner(): return lax.ppermute(value, axis, pairs)]
    pallas_call x0 -> x1, Pallas kernels: none -> 95.4 us  [shards(): pl.pallas_call(block_kernel, out_shape=jax.ShapeDtypeStruct((ROWS, COLS),...]
    ppermute x36 -> x0, starting transfers between devices: 88.4 us -> none  [from_partner(): return lax.ppermute(value, axis, pairs)]
    reduce_scatter x1 -> x0, waiting for transfers between devices: 49 us -> none  [shards(): lax.psum_scatter(partial_out, 'ch', scatter_dimension=1, tiled=True)]
    dot_general x16 -> x0, matrix products: 38.6 us -> none  [the longest x2 5.57 us: local_forward(): jnp.einsum('bj,hjc->hbc', cos_part, imag_part, precision=precise)]
    select_n x11 -> x0, other arithmetic: 34.8 us -> none  [the longest x6 31.6 us: forward_bits(): imag_part = jnp.where(upper_half, diff_imag, imag_part + recv_imag)]
  transfers between devices with their start and end apart: 37 -> 0, of which waited for: 37 -> 0; matrix products, arithmetic and copies ran while one was open for 0% -> 0% of each run, Pallas kernels for 0% -> 0%
where the time goes in v1:
time: 97.4 us; the launch traced here: 97.3 us
  Pallas kernels  95.4 us (98%)
  local copies, waits for them, and re-layouts  1.87 us (2%)
    pallas_call x1, Pallas kernels, shards(): pl.pallas_call(block_kernel, out_shape=jax.ShapeDtypeStruct((ROWS, COLS),...  95.4 us

profile of v1, /device:TPU:1, one launch (start us, length us, event | category | flops | bytes accessed | tf_op | source)
XLA Modules:
  0.0 97.3 jit_solution(10860508079148837216)
XLA Ops:
  0.0 95.4 %hyena_block.1 = bf16[256,1024]{1,0:T(8,128)(2,1)} custom-call(bf16[256,512]{1,0:T(8,128)(2,1)} %sig_ref.1, bf16[256,512]{1,0:T(8,128)(2,1)} %gate_ref.1, f32[1,512]{1,0:T(1,128)} %bitcast.4, f32[1,512]{1,0:T(1,128)} %bitcast.5, f32[33,64]{1,0:T(8,128)} %w1_ref.1, f32[1,64]{1,0:T(1,128)} %bitcast.6, f32[64,64]{1,0:T(8,128)} %w2_ref.1, f32[1,64]{1,0:T(1,128)} %bitcast.7, ...), custom_call_target="tpu_custom_call" | custom-call | tf_op jit(solution)/shard_map/hyena_block/pallas_call | solution.py:348
  95.4 1.9 %copy.13 = bf16[256,1024]{1,0:T(8,128)(2,1)} copy(bf16[256,1024]{1,0:T(8,128)(2,1)} %hyena_block.1) | data formatting | bytes 1048576

commit v2 on v1

--- a/solution.py
+++ b/solution.py
@@ -19,9 +19,10 @@
 HID = 64
 PARTS = 4
 QUARTER = SEQ_LEN // PARTS
-STEP = 256
-TAP = 64
+STEP = 1024
+TAP = 16
 DEPTH = 1024
+DEPTH_PER_PART = QUARTER // DEPTH
 TOP = SEQ_LEN - TAP
 COLS = 1024
 INV_TURN = 1.0 / (2.0 * math.pi)
@@ -99,7 +100,7 @@
     bias_ref[...] = tile_lanes(b2_ref[...]) * INV_TURN - 0.25
 
     lhs_rows = PARTS * OWN
-    pick = iota((lhs_rows, CHANS), 1) == own_first + (iota((lhs_rows, CHANS), 0) & (OWN - 1))
+    pick = iota((lhs_rows, CHANS), 1) == own_first + DEVS * (iota((lhs_rows, CHANS), 0) & (OWN - 1))
     chosen = jnp.where(pick, 1.0, 0.0).astype(BF16)
     keep = iota((lhs_rows, wide), 1) >> 6 == iota((lhs_rows, wide), 0) >> 3
     hi_part = jnp.concatenate([hi_ref[...]] * PARTS, axis=0)
@@ -140,78 +141,78 @@
         filt_ref[step * (STEP // 128) + tile] = filters[:, 128 * tile:128 * (tile + 1)]
 
 
-def toeplitz_tiles(chan, filt_ref, toep_ref):
+def toeplitz_tiles(filt_ref, toep_ref):
     shape = (TAP, 128)
     ahead = iota(shape, 1) >= iota(shape, 0)
-    inside = iota(shape, 1) <= iota(shape, 0) + TAP
-
-    def slanted(tile):
-        row = lax.div(tile, QUARTER // 128) * OWN + chan
-        taps = filt_ref[lax.rem(tile, QUARTER // 128), pl.ds(row, 1), :]
-        return pltpu.roll(jnp.broadcast_to(taps, shape), 0, 1, stride=1, stride_axis=0)
+    inside = iota(shape, 1) <= iota(shape, 0) + (128 - TAP)
+    per_part = QUARTER // 128
+
+    def slanted(part, tile):
+        taps = filt_ref[tile, pl.ds(pl.multiple_of(part * OWN, OWN), OWN), :]
+        return tuple(
+            pltpu.roll(jnp.broadcast_to(taps[chan:chan + 1], shape), 0, 1, stride=1, stride_axis=0)
+            for chan in range(OWN)
+        )
 
     def block(index, before):
+        part = lax.div(index, DEPTH_PER_PART)
+        first = lax.rem(index, DEPTH_PER_PART) * (DEPTH // 128)
         for sub in range(DEPTH // 128):
-            now = slanted(index * (DEPTH // 128) + sub)
-            tile = jnp.where(ahead, now, before)
-            if sub == DEPTH // 128 - 1:
-                tile = jnp.where(inside | (index < SEQ_LEN // DEPTH - 1), tile, 0.0)
-            toep_ref[chan, pl.ds(pl.multiple_of(index * TAP, TAP), TAP), sub * 128:(sub + 1) * 128] = tile.astype(BF16)
+            now = slanted(part, first + sub)
+            for chan in range(OWN):
+                tile = jnp.where(ahead, now[chan], before[chan])
+                if sub == DEPTH // 128 - 1:
+                    tile = jnp.where(inside | (index < SEQ_LEN // DEPTH - 1), tile, 0.0)
+                toep_ref[chan, pl.ds(pl.multiple_of(index * TAP, TAP), TAP), sub * 128:(sub + 1) * 128] = tile.astype(BF16)
             before = now
         return before
 
-    lax.fori_loop(0, SEQ_LEN // DEPTH, block, slanted(jnp.int32(SEQ_LEN // 128 - 1)))
-
-
-def shifted(value, count):
-    if count == 0:
-        return value
-    lane = iota(value.shape, 1) & 63
-    return jnp.where(lane >= count, pltpu.roll(value, count, 1), 0.0)
-
-
-def signal_columns(chan, recv_ref, cols_ref):
-    first_half = iota((64, 128), 1) < 64
-
-    def pair(tile):
-        return jnp.concatenate([tile, pltpu.roll(tile, 64, 1)], axis=0).T
-
-    low, high = (pair(recv_ref[half, pl.ds(chan, DEVS, stride=OWN), :]) for half in range(2))
-    t01, t10, t23, t32 = low[:64], low[64:], high[:64], high[64:]
-    t12 = jnp.where(first_half, t10, t32)
-    t30 = jnp.where(first_half, shifted(t32, 1), t10)
-    for back in range(DEPTH // 64):
-        whole, rem = back // 4, back % 4
-        if rem == 0:
-            left, right = shifted(t01, whole), shifted(t23, whole)
-        elif rem == 1:
-            left, right = shifted(t30, whole), shifted(t12, whole)
-        elif rem == 2:
-            left, right = shifted(t23, whole + 1), shifted(t01, whole)
-        else:
-            left, right = shifted(t12, whole + 1), shifted(t30, whole)
-        rows = slice(64 * (15 - back), 64 * (16 - back))
-        cols_ref[rows, 0:128] = left.astype(BF16)
-        cols_ref[rows, 128:256] = right.astype(BF16)
-
-
-def convolve(chan, toep_ref, cols_ref, send_ref):
-    left = jnp.zeros((64, 128), F32)
-    right = jnp.zeros((64, 128), F32)
-    for quad in range(4):
-        part = dot(toep_ref[chan, 256 * quad:256 * (quad + 1), :], cols_ref[...])
-        for sub in range(4):
-            left = shifted(left, 4) + part[64 * sub:64 * (sub + 1), 0:128]
-            right = shifted(right, 4) + part[64 * sub:64 * (sub + 1), 128:256]
-    for half, value in enumerate((left, right)):
-        turned = jnp.concatenate([value, pltpu.roll(value, 64, 1)], axis=0).T
-        send_ref[half, pl.ds(chan, DEVS, stride=OWN), :] = turned[:64]
+    lax.fori_loop(0, SEQ_LEN // DEPTH, block, slanted(PARTS - 1, per_part - 1))
+
+
+def signal_windows(chan, recv_ref, rows_ref, win_ref):
+    lane = iota((128, 128), 1)
+    before = recv_ref[pl.ds(chan, 128, stride=OWN), :]
+    after = recv_ref[pl.ds(chan + OWN, 128, stride=OWN), :]
+    for sub in range(8):
+        ahead = TAP * (sub + 1)
+        value = after
+        if ahead < 128:
+            value = pltpu.roll(jnp.where(lane >= ahead, before, after), 128 - ahead, 1)
+        rows_ref[pl.ds(56 + sub, 128, stride=8), :] = value
+    win_ref[:, 0:128] = rows_ref[0:1072, :].astype(BF16)
+    win_ref[:, 128:256] = rows_ref[8:1080, :].astype(BF16)
+
+
+def convolve(chan, toep_ref, win_ref, conv_ref):
+    sums = ([None] * 8, [None] * 8)
+    for cols in range(4):
+        window = jnp.concatenate(
+            [win_ref[16 * deep + 256 * cols:16 * deep + 256 * (cols + 1), :] for deep in range(DEPTH // 256)], axis=1
+        )
+        part = dot_nt(toep_ref[chan, 64 * cols:256, :], window)
+        for lag in range(16 - 4 * cols):
+            row = TAP * (15 - lag - 4 * cols)
+            for side in range(2):
+                tile = 2 * cols + side + lag // 2
+                if tile < 8:
+                    piece = part[row:row + TAP, 128 * side:128 * (side + 1)]
+                    old = sums[lag % 2][tile]
+                    sums[lag % 2][tile] = piece if old is None else old + piece
+    first_half = iota((TAP, 128), 1) < 64
+    earlier = jnp.zeros((TAP, 128), F32)
+    for tile in range(8):
+        turned = pltpu.roll(sums[1][tile], 64, 1)
+        conv_ref[tile, pl.ds(pl.multiple_of(chan * TAP, TAP), TAP), :] = sums[0][tile] + jnp.where(
+            first_half, earlier, turned
+        )
+        earlier = turned
 
 
 def block_kernel(sig_ref, gate_ref, skip_ref, decay_ref, w1_ref, b1_ref, w2_ref, b2_ref, hi_ref, fix_ref, wout_ref,
                  out_ref,
-                 first_ref, second_ref, bias_ref, third_ref, env_ref, filt_ref, toep_ref, cols_ref,
-                 sig_t, gate_t, recv_x, send_y, recv_y, gated_ref, wide_ref,
+                 first_ref, second_ref, bias_ref, third_ref, env_ref, filt_ref, toep_ref, rows_ref, win_ref, conv_ref,
+                 send_x, recv_x, send_y, recv_y, gated_ref, wide_ref,
                  core_send, core_recv, far_send, far_recv,
                  wide_sem, x_send_sem, x_recv_sem, y_send_sem, y_recv_sem,
                  core_send_sem, core_recv_sem, far_send_sem, far_recv_sem):
@@ -242,47 +243,53 @@
         load.start()
 
     for half in range(2):
-        part = sig_ref[128 * half:128 * (half + 1), :].astype(F32)
-        sig_t[half] = part.T
-    own_rows = pl.ds(pl.multiple_of(me * OWN, OWN), OWN)
-    recv_x[:, own_rows, :] = sig_t[:, own_rows, :]
+        turned = sig_ref[128 * half:128 * (half + 1), :].astype(F32).T
+        for chan in range(OWN):
+            send_x[pl.ds(8 * half + chan, DEVS, stride=16), :] = turned[DEVS * chan:DEVS * (chan + 1), :]
+    recv_x[0:OWN, :] = jnp.zeros((OWN, 128), F32)
+    own_send = pl.ds(pl.multiple_of(me * 16, 16), 16)
+    own_recv = pl.ds(pl.multiple_of(me * 16 + 8, 8), 16)
+    recv_x[own_recv, :] = send_x[own_send, :]
     pl.semaphore_wait(barrier, DEVS + 1)
 
     @pl.loop(1, DEVS)
     def _(step):
         peer = lax.rem(me + step, DEVS)
         pltpu.make_async_remote_copy(
-            src_ref=sig_t.at[:, pl.ds(pl.multiple_of(peer * OWN, OWN), OWN), :],
-            dst_ref=recv_x.at[:, own_rows, :],
+            src_ref=send_x.at[pl.ds(pl.multiple_of(peer * 16, 16), 16), :],
+            dst_ref=recv_x.at[own_recv, :],
             send_sem=x_send_sem,
             recv_sem=x_recv_sem,
             device_id={"seq": peer},
             device_id_type=MESH,
         ).start()
 
-    for half in range(2):
-        gate_t[half] = gate_ref[128 * half:128 * (half + 1), :].astype(F32).T
-    skip = jnp.broadcast_to(skip_ref[...], (128, CHANS)).T
-
-    filter_weights(me * OWN, decay_ref, w1_ref, b1_ref, w2_ref, b2_ref, hi_ref, fix_ref,
+    filter_weights(me, decay_ref, w1_ref, b1_ref, w2_ref, b2_ref, hi_ref, fix_ref,
                    first_ref, second_ref, bias_ref, third_ref, env_ref)
 
     @pl.loop(0, QUARTER // STEP)
     def _(step):
         filter_step(step, first_ref, second_ref, bias_ref, third_ref, env_ref, filt_ref)
 
-    @pl.loop(0, OWN)
+    toeplitz_tiles(filt_ref, toep_ref)
+
+    rows_ref[0:56, :] = jnp.zeros((56, 128), F32)
+    many = pl.ds(0, (DEVS - 1) * 16)
+    pltpu.make_async_copy(recv_x.at[many, :], recv_x.at[many, :], x_recv_sem).wait()
+
+    @pl.loop(0, OWN, unroll=2)
     def _(chan):
-        toeplitz_tiles(chan, filt_ref, toep_ref)
-
-    many = pl.ds(0, (DEVS - 1) * OWN)
-    pltpu.make_async_copy(recv_x.at[:, many, :], recv_x.at[:, many, :], x_recv_sem).wait()
-
-    @pl.loop(0, OWN)
-    def _(chan):
-        signal_columns(chan, recv_x, cols_ref)
-        convolve(chan, toep_ref, cols_ref, send_y)
-
+        signal_windows(chan, recv_x, rows_ref, win_ref)
+        convolve(chan, toep_ref, win_ref, conv_ref)
+
+    for tile in range(8):
+        turned = conv_ref[tile].T
+        for peer in range(8):
+            for half in range(2):
+                send_y[half, 64 * tile + 8 * peer:64 * tile + 8 * (peer + 1), :] = (
+                    turned[16 * peer + 8 * half:16 * peer + 8 * (half + 1), :]
+                )
+    own_rows = pl.ds(pl.multiple_of(me * 8, 8), 8)
     for half in range(2):
         recv_y[half, own_rows, :] = send_y[half, own_rows, :]
 
@@ -290,7 +297,7 @@
         def _(step):
             peer = lax.rem(me + step, DEVS)
             pltpu.make_async_remote_copy(
-                src_ref=send_y.at[half, pl.ds(pl.multiple_of(peer * OWN, OWN), OWN), :],
+                src_ref=send_y.at[half, pl.ds(pl.multiple_of(peer * 8, 8), 8), :],
                 dst_ref=recv_y.at[half, own_rows, :],
                 send_sem=y_send_sem.at[half],
                 recv_sem=y_recv_sem.at[half],
@@ -314,10 +321,28 @@
 
     for load in loads:
         load.wait()
+    half_rows = pl.ds(0, (DEVS - 1) * 8)
+    first_half = iota((16, 128), 1) < 64
     for half in range(2):
-        pltpu.make_async_copy(recv_y.at[half, many, :], recv_y.at[half, many, :], y_recv_sem.at[half]).wait()
-        gated = gate_t[half] * (recv_y[half] + skip * sig_t[half])
-        gated_ref[...] = gated.T.astype(BF16)
+        pltpu.make_async_copy(recv_y.at[half, half_rows, :], recv_y.at[half, half_rows, :], y_recv_sem.at[half]).wait()
+        for pair in range(4):
+            both = jnp.concatenate(
+                [recv_y[half, pl.ds(2 * pair + side, DEVS, stride=8), :] for side in range(2)], axis=0
+            ).T
+            swapped = pltpu.roll(both, 64, 1)
+            for two in range(OWN // 2):
+                low = slice(32 * two, 32 * two + 16)
+                high = slice(32 * two + 16, 32 * two + 32)
+                lanes = slice(128 * two, 128 * (two + 1))
+                for side, value in enumerate((
+                    jnp.where(first_half, both[low], swapped[high]), jnp.where(first_half, swapped[low], both[high])
+                )):
+                    place = 16 * (2 * pair + side)
+                    rows = slice(128 * half + place, 128 * half + place + 16)
+                    gated_ref[place:place + 16, lanes] = (
+                        gate_ref[rows, lanes].astype(F32)
+                        * (value + skip_ref[:, lanes] * sig_ref[rows, lanes].astype(F32))
+                    ).astype(BF16)
         core_send[half, 0] = dot(gated_ref[...], wide_ref[0])
         to_core(half, 0).start()
         far_send[half] = dot(gated_ref[...], wide_ref[1])
@@ -333,9 +358,9 @@
         to_far(half).wait_recv()
         out_ref[128 * half:128 * (half + 1), :] = (core_recv[half, 1] + far_recv[half]).astype(BF16)
 
-    pltpu.make_async_copy(sig_t.at[:, many, :], sig_t.at[:, many, :], x_send_sem).wait()
+    pltpu.make_async_copy(send_x.at[many, :], send_x.at[many, :], x_send_sem).wait()
     for half in range(2):
-        pltpu.make_async_copy(send_y.at[half, many, :], send_y.at[half, many, :], y_send_sem.at[half]).wait()
+        pltpu.make_async_copy(send_y.at[half, half_rows, :], send_y.at[half, half_rows, :], y_send_sem.at[half]).wait()
         for which in range(2):
             to_core(half, which).wait_send()
         to_far(half).wait_send()
@@ -358,12 +383,13 @@
             pltpu.VMEM((PARTS * OWN, 128), F32),
             pltpu.VMEM((QUARTER // 128, PARTS * OWN, 128), F32),
             pltpu.VMEM((OWN, SEQ_LEN // DEPTH * TAP, DEPTH), BF16),
-            pltpu.VMEM((DEPTH, 256), BF16),
-            pltpu.VMEM((2, CHANS, 128), F32),
-            pltpu.VMEM((2, CHANS, 128), F32),
-            pltpu.VMEM((2, CHANS, 128), F32),
-            pltpu.VMEM((2, CHANS, 128), F32),
-            pltpu.VMEM((2, CHANS, 128), F32),
+            pltpu.VMEM((1088, 128), F32),
+            pltpu.VMEM((1072, 256), BF16),
+            pltpu.VMEM((8, 128, 128), F32),
+            pltpu.VMEM((DEVS * 16, 128), F32),
+            pltpu.VMEM((DEVS * 16 + 8, 128), F32),
+            pltpu.VMEM((2, DEVS * 8, 128), F32),
+            pltpu.VMEM((2, DEVS * 8, 128), F32),
             pltpu.VMEM((128, CHANS), BF16),
             pltpu.VMEM((4, CHANS, COLS), BF16),
             pltpu.VMEM((2, 2, 128, COLS), F32),

time: 97.4 us -> 74.9 us (0.77)
  Pallas kernels: 95.4 us -> 72.9 us
    pallas_call x1, Pallas kernels: 95.4 us -> 72.9 us  [shards(): pl.pallas_call(block_kernel, out_shape=jax.ShapeDtypeStruct((ROWS, COLS),...]
where the time goes in v2:
time: 74.9 us; the launch traced here: 74.8 us
  Pallas kernels  72.9 us (97%)
  local copies, waits for them, and re-layouts  1.87 us (2%)
    pallas_call x1, Pallas kernels, shards(): pl.pallas_call(block_kernel, out_shape=jax.ShapeDtypeStruct((ROWS, COLS),...  72.9 us
    unnamed x1, local copies, waits for them, and re-layouts  1.87 us

profile of v2, /device:TPU:1, one launch (start us, length us, event | category | flops | bytes accessed | tf_op | source)
XLA Modules:
  0.0 74.8 jit_solution(5519091073350829997)
XLA Ops:
  0.0 72.9 %hyena_block.1 = bf16[256,1024]{1,0:T(8,128)(2,1)} custom-call(bf16[256,512]{1,0:T(8,128)(2,1)} %sig_ref.1, bf16[256,512]{1,0:T(8,128)(2,1)} %gate_ref.1, f32[1,512]{1,0:T(1,128)} %bitcast.4, f32[1,512]{1,0:T(1,128)} %bitcast.5, f32[33,64]{1,0:T(8,128)} %w1_ref.1, f32[1,64]{1,0:T(1,128)} %bitcast.6, f32[64,64]{1,0:T(8,128)} %w2_ref.1, f32[1,64]{1,0:T(1,128)} %bitcast.7, ...), custom_call_target="tpu_custom_call" | custom-call | tf_op jit(solution)/shard_map/hyena_block/pallas_call | solution.py:373
  72.9 1.9 %copy.13 = bf16[256,1024]{1,0:T(8,128)(2,1)} copy(bf16[256,1024]{1,0:T(8,128)(2,1)} %hyena_block.1) | data formatting | bytes 1048576

commit v3 on v2

--- a/solution.py
+++ b/solution.py
@@ -212,7 +212,7 @@
 def block_kernel(sig_ref, gate_ref, skip_ref, decay_ref, w1_ref, b1_ref, w2_ref, b2_ref, hi_ref, fix_ref, wout_ref,
                  out_ref,
                  first_ref, second_ref, bias_ref, third_ref, env_ref, filt_ref, toep_ref, rows_ref, win_ref, conv_ref,
-                 send_x, recv_x, send_y, recv_y, gated_ref, wide_ref,
+                 send_x, recv_x, send_y, recv_y, gated_ref, wide_ref, total_ref,
                  core_send, core_recv, far_send, far_recv,
                  wide_sem, x_send_sem, x_recv_sem, y_send_sem, y_recv_sem,
                  core_send_sem, core_recv_sem, far_send_sem, far_recv_sem):
@@ -285,49 +285,51 @@
     for tile in range(8):
         turned = conv_ref[tile].T
         for peer in range(8):
-            for half in range(2):
-                send_y[half, 64 * tile + 8 * peer:64 * tile + 8 * (peer + 1), :] = (
-                    turned[16 * peer + 8 * half:16 * peer + 8 * (half + 1), :]
-                )
-    own_rows = pl.ds(pl.multiple_of(me * 8, 8), 8)
-    for half in range(2):
-        recv_y[half, own_rows, :] = send_y[half, own_rows, :]
+            for quarter in range(4):
+                place = 32 * tile + 4 * peer
+                row = 16 * peer + 4 * quarter
+                send_y[quarter, place:place + 4, :] = turned[row:row + 4, :]
+    own_rows = pl.ds(pl.multiple_of(me * 4, 4), 4)
+    for quarter in range(4):
+        recv_y[quarter, own_rows, :] = send_y[quarter, own_rows, :]
 
         @pl.loop(1, DEVS)
         def _(step):
             peer = lax.rem(me + step, DEVS)
             pltpu.make_async_remote_copy(
-                src_ref=send_y.at[half, pl.ds(pl.multiple_of(peer * 8, 8), 8), :],
-                dst_ref=recv_y.at[half, own_rows, :],
-                send_sem=y_send_sem.at[half],
-                recv_sem=y_recv_sem.at[half],
+                src_ref=send_y.at[quarter, pl.ds(pl.multiple_of(peer * 4, 4), 4), :],
+                dst_ref=recv_y.at[quarter, own_rows, :],
+                send_sem=y_send_sem.at[quarter],
+                recv_sem=y_recv_sem.at[quarter],
                 device_id={"seq": peer},
                 device_id_type=MESH,
             ).start()
 
-    def to_core(half, which):
+    def to_core(quarter, which):
         return pltpu.make_async_remote_copy(
-            src_ref=core_send.at[half, which], dst_ref=core_recv.at[half, which],
-            send_sem=core_send_sem.at[half, which], recv_sem=core_recv_sem.at[half, which],
+            src_ref=core_send.at[quarter, which], dst_ref=core_recv.at[quarter, which],
+            send_sem=core_send_sem.at[quarter, which], recv_sem=core_recv_sem.at[quarter, which],
             device_id={"ch": core_mate}, device_id_type=MESH,
         )
 
-    def to_far(half):
+    def to_far(quarter):
         return pltpu.make_async_remote_copy(
-            src_ref=far_send.at[half], dst_ref=far_recv.at[half],
-            send_sem=far_send_sem.at[half], recv_sem=far_recv_sem.at[half],
+            src_ref=far_send.at[quarter], dst_ref=far_recv.at[quarter],
+            send_sem=far_send_sem.at[quarter], recv_sem=far_recv_sem.at[quarter],
             device_id={"ch": far_mate}, device_id_type=MESH,
         )
 
     for load in loads:
         load.wait()
-    half_rows = pl.ds(0, (DEVS - 1) * 8)
+    part_rows = pl.ds(0, (DEVS - 1) * 4)
     first_half = iota((16, 128), 1) < 64
-    for half in range(2):
-        pltpu.make_async_copy(recv_y.at[half, half_rows, :], recv_y.at[half, half_rows, :], y_recv_sem.at[half]).wait()
-        for pair in range(4):
+    for quarter in range(4):
+        pltpu.make_async_copy(
+            recv_y.at[quarter, part_rows, :], recv_y.at[quarter, part_rows, :], y_recv_sem.at[quarter]
+        ).wait()
+        for pair in range(2):
             both = jnp.concatenate(
-                [recv_y[half, pl.ds(2 * pair + side, DEVS, stride=8), :] for side in range(2)], axis=0
+                [recv_y[quarter, pl.ds(2 * pair + side, DEVS, stride=4), :] for side in range(2)], axis=0
             ).T
             swapped = pltpu.roll(both, 64, 1)
             for two in range(OWN // 2):
@@ -338,32 +340,35 @@
                     jnp.where(first_half, both[low], swapped[high]), jnp.where(first_half, swapped[low], both[high])
                 )):
                     place = 16 * (2 * pair + side)
-                    rows = slice(128 * half + place, 128 * half + place + 16)
+                    rows = slice(64 * quarter + place, 64 * quarter + place + 16)
                     gated_ref[place:place + 16, lanes] = (
                         gate_ref[rows, lanes].astype(F32)
                         * (value + skip_ref[:, lanes] * sig_ref[rows, lanes].astype(F32))
                     ).astype(BF16)
-        core_send[half, 0] = dot(gated_ref[...], wide_ref[0])
-        to_core(half, 0).start()
-        far_send[half] = dot(gated_ref[...], wide_ref[1])
-        to_core(half, 0).wait_recv()
-        far_send[half] += core_recv[half, 0]
-        to_far(half).start()
-        core_send[half, 1] = dot(gated_ref[...], wide_ref[2])
-        to_core(half, 1).start()
-        total = dot(gated_ref[...], wide_ref[3])
-        to_core(half, 1).wait_recv()
-        core_recv[half, 1] += total
-    for half in range(2):
-        to_far(half).wait_recv()
-        out_ref[128 * half:128 * (half + 1), :] = (core_recv[half, 1] + far_recv[half]).astype(BF16)
+        core_send[quarter, 0] = dot(gated_ref[...], wide_ref[0])
+        to_core(quarter, 0).start()
+        far_send[quarter] = dot(gated_ref[...], wide_ref[1])
+        to_core(quarter, 0).wait_recv()
+        far_send[quarter] += core_recv[quarter, 0]
+        to_far(quarter).start()
+        core_send[quarter, 1] = dot(gated_ref[...], wide_ref[2])
+        to_core(quarter, 1).start()
+        total_ref[quarter] = dot(gated_ref[...], wide_ref[3])
+    for quarter in range(4):
+        to_core(quarter, 1).wait_recv()
+        to_far(quarter).wait_recv()
+        out_ref[64 * quarter:64 * (quarter + 1), :] = (
+            total_ref[quarter] + core_recv[quarter, 1] + far_recv[quarter]
+        ).astype(BF16)
 
     pltpu.make_async_copy(send_x.at[many, :], send_x.at[many, :], x_send_sem).wait()
-    for half in range(2):
-        pltpu.make_async_copy(send_y.at[half, half_rows, :], send_y.at[half, half_rows, :], y_send_sem.at[half]).wait()
+    for quarter in range(4):
+        pltpu.make_async_copy(
+            send_y.at[quarter, part_rows, :], send_y.at[quarter, part_rows, :], y_send_sem.at[quarter]
+        ).wait()
         for which in range(2):
-            to_core(half, which).wait_send()
-        to_far(half).wait_send()
+            to_core(quarter, which).wait_send()
+        to_far(quarter).wait_send()
 
 
 def shards(signal, gate_in, skip_gain, decay, pos_weight1, pos_bias1, pos_weight2, pos_bias2, filt_hi, filt_fix,
@@ -388,23 +393,24 @@
             pltpu.VMEM((8, 128, 128), F32),
             pltpu.VMEM((DEVS * 16, 128), F32),
             pltpu.VMEM((DEVS * 16 + 8, 128), F32),
-            pltpu.VMEM((2, DEVS * 8, 128), F32),
-            pltpu.VMEM((2, DEVS * 8, 128), F32),
-            pltpu.VMEM((128, CHANS), BF16),
+            pltpu.VMEM((4, DEVS * 4, 128), F32),
+            pltpu.VMEM((4, DEVS * 4, 128), F32),
+            pltpu.VMEM((64, CHANS), BF16),
             pltpu.VMEM((4, CHANS, COLS), BF16),
-            pltpu.VMEM((2, 2, 128, COLS), F32),
-            pltpu.VMEM((2, 2, 128, COLS), F32),
-            pltpu.VMEM((2, 128, COLS), F32),
-            pltpu.VMEM((2, 128, COLS), F32),
+            pltpu.VMEM((4, 64, COLS), F32),
+            pltpu.VMEM((4, 2, 64, COLS), F32),
+            pltpu.VMEM((4, 2, 64, COLS), F32),
+            pltpu.VMEM((4, 64, COLS), F32),
+            pltpu.VMEM((4, 64, COLS), F32),
             pltpu.SemaphoreType.DMA((4,)),
             pltpu.SemaphoreType.DMA,
             pltpu.SemaphoreType.DMA,
-            pltpu.SemaphoreType.DMA((2,)),
-            pltpu.SemaphoreType.DMA((2,)),
-            pltpu.SemaphoreType.DMA((2, 2)),
-            pltpu.SemaphoreType.DMA((2, 2)),
-            pltpu.SemaphoreType.DMA((2,)),
-            pltpu.SemaphoreType.DMA((2,)),
+            pltpu.SemaphoreType.DMA((4,)),
+            pltpu.SemaphoreType.DMA((4,)),
+            pltpu.SemaphoreType.DMA((4, 2)),
+            pltpu.SemaphoreType.DMA((4, 2)),
+            pltpu.SemaphoreType.DMA((4,)),
+            pltpu.SemaphoreType.DMA((4,)),
         ],
         compiler_params=pltpu.CompilerParams(
             collective_id=0, has_side_effects=True, vmem_limit_bytes=56 * 2**20

time: 74.9 us -> 73.1 us (0.976)
  Pallas kernels: 72.9 us -> 71.1 us
    pallas_call x1, Pallas kernels: 72.9 us -> 71.1 us  [shards(): pl.pallas_call(block_kernel, out_shape=jax.ShapeDtypeStruct((ROWS, COLS),...]
where the time goes in v3:
time: 73.1 us; the launch traced here: 72.9 us
  Pallas kernels  71.1 us (97%)
  local copies, waits for them, and re-layouts  1.87 us (3%)
    pallas_call x1, Pallas kernels, shards(): pl.pallas_call(block_kernel, out_shape=jax.ShapeDtypeStruct((ROWS, COLS),...  71.1 us
    unnamed x1, local copies, waits for them, and re-layouts  1.87 us

profile of v3, /device:TPU:1, one launch (start us, length us, event | category | flops | bytes accessed | tf_op | source)
XLA Modules:
  0.0 72.9 jit_solution(6569214973258184342)
XLA Ops:
  0.0 71.1 %hyena_block.1 = bf16[256,1024]{1,0:T(8,128)(2,1)} custom-call(bf16[256,512]{1,0:T(8,128)(2,1)} %sig_ref.1, bf16[256,512]{1,0:T(8,128)(2,1)} %gate_ref.1, f32[1,512]{1,0:T(1,128)} %bitcast.4, f32[1,512]{1,0:T(1,128)} %bitcast.5, f32[33,64]{1,0:T(8,128)} %w1_ref.1, f32[1,64]{1,0:T(1,128)} %bitcast.6, f32[64,64]{1,0:T(8,128)} %w2_ref.1, f32[1,64]{1,0:T(1,128)} %bitcast.7, ...), custom_call_target="tpu_custom_call" | custom-call | tf_op jit(solution)/shard_map/hyena_block/pallas_call | solution.py:378
  71.1 1.9 %copy.13 = bf16[256,1024]{1,0:T(8,128)(2,1)} copy(bf16[256,1024]{1,0:T(8,128)(2,1)} %hyena_block.1) | data formatting | bytes 1048576

commit v4 on v3

--- a/solution.py
+++ b/solution.py
@@ -16,6 +16,7 @@
 ROWS = 256
 CHANS = 512
 OWN = 8
+SUB = 4
 HID = 64
 PARTS = 4
 QUARTER = SEQ_LEN // PARTS
@@ -172,8 +173,8 @@
 
 def signal_windows(chan, recv_ref, rows_ref, win_ref):
     lane = iota((128, 128), 1)
-    before = recv_ref[pl.ds(chan, 128, stride=OWN), :]
-    after = recv_ref[pl.ds(chan + OWN, 128, stride=OWN), :]
+    before = recv_ref[pl.ds(SUB + chan, 128, stride=SUB), :]
+    after = recv_ref[pl.ds(2 * SUB + chan, 128, stride=SUB), :]
     for sub in range(8):
         ahead = TAP * (sub + 1)
         value = after
@@ -212,10 +213,10 @@
 def block_kernel(sig_ref, gate_ref, skip_ref, decay_ref, w1_ref, b1_ref, w2_ref, b2_ref, hi_ref, fix_ref, wout_ref,
                  out_ref,
                  first_ref, second_ref, bias_ref, third_ref, env_ref, filt_ref, toep_ref, rows_ref, win_ref, conv_ref,
-                 send_x, recv_x, send_y, recv_y, gated_ref, wide_ref, total_ref,
+                 send_x, recv_x, send_y, recv_y, gated_ref, wide_ref, total_ref, mixed_ref,
                  core_send, core_recv, far_send, far_recv,
                  wide_sem, x_send_sem, x_recv_sem, y_send_sem, y_recv_sem,
-                 core_send_sem, core_recv_sem, far_send_sem, far_recv_sem):
+                 core_send_sem, core_recv_sem, far_send_sem, far_recv_sem, out_sem):
     me = lax.axis_index("seq")
     group = lax.axis_index("ch")
     core = lax.rem(group, 2)
@@ -245,24 +246,29 @@
     for half in range(2):
         turned = sig_ref[128 * half:128 * (half + 1), :].astype(F32).T
         for chan in range(OWN):
-            send_x[pl.ds(8 * half + chan, DEVS, stride=16), :] = turned[DEVS * chan:DEVS * (chan + 1), :]
-    recv_x[0:OWN, :] = jnp.zeros((OWN, 128), F32)
-    own_send = pl.ds(pl.multiple_of(me * 16, 16), 16)
-    own_recv = pl.ds(pl.multiple_of(me * 16 + 8, 8), 16)
-    recv_x[own_recv, :] = send_x[own_send, :]
+            send_x[chan // SUB, pl.ds(SUB * half + chan % SUB, DEVS, stride=8), :] = (
+                turned[DEVS * chan:DEVS * (chan + 1), :]
+            )
+    own_send = pl.ds(pl.multiple_of(me * 8, 8), 8)
+    own_recv = pl.ds(pl.multiple_of(me * 8 + 8, 8), 8)
+    for group_num in range(2):
+        recv_x[group_num, 0:8, :] = jnp.zeros((8, 128), F32)
+        recv_x[group_num, own_recv, :] = send_x[group_num, own_send, :]
     pl.semaphore_wait(barrier, DEVS + 1)
 
-    @pl.loop(1, DEVS)
-    def _(step):
-        peer = lax.rem(me + step, DEVS)
-        pltpu.make_async_remote_copy(
-            src_ref=send_x.at[pl.ds(pl.multiple_of(peer * 16, 16), 16), :],
-            dst_ref=recv_x.at[own_recv, :],
-            send_sem=x_send_sem,
-            recv_sem=x_recv_sem,
-            device_id={"seq": peer},
-            device_id_type=MESH,
-        ).start()
+    for group_num in range(2):
+
+        @pl.loop(1, DEVS)
+        def _(step):
+            peer = lax.rem(me + step, DEVS)
+            pltpu.make_async_remote_copy(
+                src_ref=send_x.at[group_num, pl.ds(pl.multiple_of(peer * 8, 8), 8), :],
+                dst_ref=recv_x.at[group_num, own_recv, :],
+                send_sem=x_send_sem.at[group_num],
+                recv_sem=x_recv_sem.at[group_num],
+                device_id={"seq": peer},
+                device_id_type=MESH,
+            ).start()
 
     filter_weights(me, decay_ref, w1_ref, b1_ref, w2_ref, b2_ref, hi_ref, fix_ref,
                    first_ref, second_ref, bias_ref, third_ref, env_ref)
@@ -274,13 +280,16 @@
     toeplitz_tiles(filt_ref, toep_ref)
 
     rows_ref[0:56, :] = jnp.zeros((56, 128), F32)
-    many = pl.ds(0, (DEVS - 1) * 16)
-    pltpu.make_async_copy(recv_x.at[many, :], recv_x.at[many, :], x_recv_sem).wait()
-
-    @pl.loop(0, OWN, unroll=2)
-    def _(chan):
-        signal_windows(chan, recv_x, rows_ref, win_ref)
-        convolve(chan, toep_ref, win_ref, conv_ref)
+    many = pl.ds(0, (DEVS - 1) * 8)
+    for group_num in range(2):
+        pltpu.make_async_copy(
+            recv_x.at[group_num, many, :], recv_x.at[group_num, many, :], x_recv_sem.at[group_num]
+        ).wait()
+
+        @pl.loop(0, SUB, unroll=2)
+        def _(chan):
+            signal_windows(chan, recv_x.at[group_num], rows_ref, win_ref)
+            convolve(group_num * SUB + chan, toep_ref, win_ref, conv_ref)
 
     for tile in range(8):
         turned = conv_ref[tile].T
@@ -317,6 +326,11 @@
             src_ref=far_send.at[quarter], dst_ref=far_recv.at[quarter],
             send_sem=far_send_sem.at[quarter], recv_sem=far_recv_sem.at[quarter],
             device_id={"ch": far_mate}, device_id_type=MESH,
+        )
+
+    def to_out(quarter):
+        return pltpu.make_async_copy(
+            mixed_ref.at[quarter], out_ref.at[64 * quarter:64 * (quarter + 1), :], out_sem.at[quarter]
         )
 
     for load in loads:
@@ -357,11 +371,15 @@
     for quarter in range(4):
         to_core(quarter, 1).wait_recv()
         to_far(quarter).wait_recv()
-        out_ref[64 * quarter:64 * (quarter + 1), :] = (
-            total_ref[quarter] + core_recv[quarter, 1] + far_recv[quarter]
-        ).astype(BF16)
-
-    pltpu.make_async_copy(send_x.at[many, :], send_x.at[many, :], x_send_sem).wait()
+        mixed_ref[quarter] = (total_ref[quarter] + core_recv[quarter, 1] + far_recv[quarter]).astype(BF16)
+        to_out(quarter).start()
+    for quarter in range(4):
+        to_out(quarter).wait()
+
+    for group_num in range(2):
+        pltpu.make_async_copy(
+            send_x.at[group_num, many, :], send_x.at[group_num, many, :], x_send_sem.at[group_num]
+        ).wait()
     for quarter in range(4):
         pltpu.make_async_copy(
             send_y.at[quarter, part_rows, :], send_y.at[quarter, part_rows, :], y_send_sem.at[quarter]
@@ -379,7 +397,7 @@
         block_kernel,
         out_shape=jax.ShapeDtypeStruct((ROWS, COLS), BF16),
         in_specs=[vmem] * 10 + [pl.BlockSpec(memory_space=pl.ANY)],
-        out_specs=vmem,
+        out_specs=pl.BlockSpec(memory_space=pl.ANY),
         scratch_shapes=[
             pltpu.VMEM((128, wide), BF16),
             pltpu.VMEM((2, wide, wide), BF16),
@@ -391,24 +409,26 @@
             pltpu.VMEM((1088, 128), F32),
             pltpu.VMEM((1072, 256), BF16),
             pltpu.VMEM((8, 128, 128), F32),
-            pltpu.VMEM((DEVS * 16, 128), F32),
-            pltpu.VMEM((DEVS * 16 + 8, 128), F32),
+            pltpu.VMEM((2, DEVS * 8, 128), F32),
+            pltpu.VMEM((2, DEVS * 8 + 8, 128), F32),
             pltpu.VMEM((4, DEVS * 4, 128), F32),
             pltpu.VMEM((4, DEVS * 4, 128), F32),
             pltpu.VMEM((64, CHANS), BF16),
             pltpu.VMEM((4, CHANS, COLS), BF16),
             pltpu.VMEM((4, 64, COLS), F32),
+            pltpu.VMEM((4, 64, COLS), BF16),
             pltpu.VMEM((4, 2, 64, COLS), F32),
             pltpu.VMEM((4, 2, 64, COLS), F32),
             pltpu.VMEM((4, 64, COLS), F32),
             pltpu.VMEM((4, 64, COLS), F32),
             pltpu.SemaphoreType.DMA((4,)),
-            pltpu.SemaphoreType.DMA,
-            pltpu.SemaphoreType.DMA,
+            pltpu.SemaphoreType.DMA((2,)),
+            pltpu.SemaphoreType.DMA((2,)),
             pltpu.SemaphoreType.DMA((4,)),
             pltpu.SemaphoreType.DMA((4,)),
             pltpu.SemaphoreType.DMA((4, 2)),
             pltpu.SemaphoreType.DMA((4, 2)),
+            pltpu.SemaphoreType.DMA((4,)),
             pltpu.SemaphoreType.DMA((4,)),
             pltpu.SemaphoreType.DMA((4,)),
         ],

time: 73.1 us -> 71.4 us (0.977)
  Pallas kernels: 71.1 us -> 69.4 us
    pallas_call x1, Pallas kernels: 71.1 us -> 69.4 us  [shards(): pl.pallas_call(block_kernel, out_shape=jax.ShapeDtypeStruct((ROWS, COLS),...]
where the time goes in v4:
time: 71.4 us; the launch traced here: 71.3 us
  Pallas kernels  69.4 us (97%)
  local copies, waits for them, and re-layouts  1.87 us (3%)
    pallas_call x1, Pallas kernels, shards(): pl.pallas_call(block_kernel, out_shape=jax.ShapeDtypeStruct((ROWS, COLS),...  69.4 us
    unnamed x1, local copies, waits for them, and re-layouts  1.87 us

profile of v4, /device:TPU:1, one launch (start us, length us, event | category | flops | bytes accessed | tf_op | source)
XLA Modules:
  0.0 71.3 jit_solution(8087362383036715128)
XLA Ops:
  0.0 69.4 %hyena_block.1 = bf16[256,1024]{1,0:T(8,128)(2,1)} custom-call(bf16[256,512]{1,0:T(8,128)(2,1)} %sig_ref.1, bf16[256,512]{1,0:T(8,128)(2,1)} %gate_ref.1, f32[1,512]{1,0:T(1,128)} %bitcast.4, f32[1,512]{1,0:T(1,128)} %bitcast.5, f32[33,64]{1,0:T(8,128)} %w1_ref.1, f32[1,64]{1,0:T(1,128)} %bitcast.6, f32[64,64]{1,0:T(8,128)} %w2_ref.1, f32[1,64]{1,0:T(1,128)} %bitcast.7, ...), custom_call_target="tpu_custom_call" | custom-call | tf_op jit(solution)/shard_map/hyena_block/pallas_call | solution.py:396
  69.4 1.9 %copy.13 = bf16[256,1024]{1,0:T(8,128)(2,1)} copy(bf16[256,1024]{1,0:T(8,128)(2,1)} %hyena_block.1) | data formatting | bytes 1048576

commit v5 on v4

--- a/solution.py
+++ b/solution.py
@@ -115,15 +115,15 @@
 
 
 def filter_step(step, first_ref, second_ref, bias_ref, third_ref, env_ref, filt_ref):
-    lane = iota((STEP, 128), 1)
+    lane = iota((1, 128), 1)
     where_in = (iota((STEP, 128), 0) + step * STEP).astype(F32)
-    freq = ((lane & 15) + 1).astype(F32)
+    rate = ((lane & 15) + 1).astype(F32) * (1.0 / SEQ_LEN)
     shift = jnp.where((lane & 16) == 0, 0.0, 0.25)
-    value = turn_cos(where_in * freq * (1.0 / SEQ_LEN) - shift)
-    value = jnp.where(lane < 96, value, where_in * (1.0 / QUARTER))
-    value = jnp.where(lane < 100, value, 1.0)
-    value = jnp.where(lane < 103, value, jnp.where(where_in > TOP - QUARTER * (PARTS - 1), 1.0, 0.0))
-    value = jnp.where(lane < 106, value, 0.0)
+    slope = jnp.where(lane < 100, 1.0 / QUARTER, 0.0)
+    start = jnp.where((lane >= 100) & (lane < 103), 1.0, 0.0)
+    turn = jnp.where((lane >= 103) & (lane < 106), float(TOP - QUARTER * (PARTS - 1)), float(SEQ_LEN))
+    value = jnp.where(lane < 96, turn_cos(where_in * rate - shift), where_in * slope + start)
+    value = jnp.where(where_in > turn, 1.0, value)
     low = ((lane >= 32) & (lane < 64)) | (lane == 97) | (lane == 99)
     high = value.astype(BF16).astype(F32)
     feats = jnp.where(low, value - high, high).astype(BF16)
@@ -185,7 +185,7 @@
     win_ref[:, 128:256] = rows_ref[8:1080, :].astype(BF16)
 
 
-def convolve(chan, toep_ref, win_ref, conv_ref):
+def convolve(chan, place, toep_ref, win_ref, conv_ref):
     sums = ([None] * 8, [None] * 8)
     for cols in range(4):
         window = jnp.concatenate(
@@ -204,7 +204,7 @@
     earlier = jnp.zeros((TAP, 128), F32)
     for tile in range(8):
         turned = pltpu.roll(sums[1][tile], 64, 1)
-        conv_ref[tile, pl.ds(pl.multiple_of(chan * TAP, TAP), TAP), :] = sums[0][tile] + jnp.where(
+        conv_ref[tile, pl.ds(pl.multiple_of(place * TAP, TAP), TAP), :] = sums[0][tile] + jnp.where(
             first_half, earlier, turned
         )
         earlier = turned
@@ -213,7 +213,7 @@
 def block_kernel(sig_ref, gate_ref, skip_ref, decay_ref, w1_ref, b1_ref, w2_ref, b2_ref, hi_ref, fix_ref, wout_ref,
                  out_ref,
                  first_ref, second_ref, bias_ref, third_ref, env_ref, filt_ref, toep_ref, rows_ref, win_ref, conv_ref,
-                 send_x, recv_x, send_y, recv_y, gated_ref, wide_ref, total_ref, mixed_ref,
+                 send_x, recv_x, turn_ref, send_y0, send_y1, send_y2, recv_y0, recv_y1, recv_y2, gated_ref, wide_ref, total_ref, mixed_ref,
                  core_send, core_recv, far_send, far_recv,
                  wide_sem, x_send_sem, x_recv_sem, y_send_sem, y_recv_sem,
                  core_send_sem, core_recv_sem, far_send_sem, far_recv_sem, out_sem):
@@ -254,6 +254,8 @@
     for group_num in range(2):
         recv_x[group_num, 0:8, :] = jnp.zeros((8, 128), F32)
         recv_x[group_num, own_recv, :] = send_x[group_num, own_send, :]
+    filter_weights(me, decay_ref, w1_ref, b1_ref, w2_ref, b2_ref, hi_ref, fix_ref,
+                   first_ref, second_ref, bias_ref, third_ref, env_ref)
     pl.semaphore_wait(barrier, DEVS + 1)
 
     for group_num in range(2):
@@ -270,9 +272,6 @@
                 device_id_type=MESH,
             ).start()
 
-    filter_weights(me, decay_ref, w1_ref, b1_ref, w2_ref, b2_ref, hi_ref, fix_ref,
-                   first_ref, second_ref, bias_ref, third_ref, env_ref)
-
     @pl.loop(0, QUARTER // STEP)
     def _(step):
         filter_step(step, first_ref, second_ref, bias_ref, third_ref, env_ref, filt_ref)
@@ -280,6 +279,49 @@
     toeplitz_tiles(filt_ref, toep_ref)
 
     rows_ref[0:56, :] = jnp.zeros((56, 128), F32)
+    pieces = ((0, 0, 8), (1, 0, 2), (1, 2, 6))
+    outgoing, incoming = (send_y0, send_y1, send_y2), (recv_y0, recv_y1, recv_y2)
+
+    def own_piece(size):
+        return pl.ds(pl.multiple_of(me * size, 2), size)
+
+    def return_rows(group_num):
+        even_half = iota((64, 128), 1) < 64
+        for tile in range(8):
+            value = conv_ref[group_num, tile]
+            turn_ref[tile] = jnp.concatenate([value, value], axis=0).T
+            block = jnp.where(
+                even_half, turn_ref[tile, pl.ds(0, 64, stride=2), :], turn_ref[tile, pl.ds(1, 64, stride=2), :]
+            )
+            for slot, (which, first, size) in enumerate(pieces):
+                if which == group_num:
+                    if size == 8:
+                        outgoing[slot][64 * tile:64 * (tile + 1), :] = block
+                    else:
+                        for peer in range(8):
+                            place = (8 * tile + peer) * size
+                            row = 8 * peer + first
+                            outgoing[slot][place:place + size, :] = block[row:row + size, :]
+        for slot, (which, _, size) in enumerate(pieces):
+            if which == group_num:
+                incoming[slot][own_piece(size), :] = outgoing[slot][own_piece(size), :]
+
+                @pl.loop(1, DEVS)
+                def _(step):
+                    peer = lax.rem(me + step, DEVS)
+                    pltpu.make_async_remote_copy(
+                        src_ref=outgoing[slot].at[pl.ds(pl.multiple_of(peer * size, 2), size), :],
+                        dst_ref=incoming[slot].at[own_piece(size), :],
+                        send_sem=y_send_sem.at[slot],
+                        recv_sem=y_recv_sem.at[slot],
+                        device_id={"seq": peer},
+                        device_id_type=MESH,
+                    ).start()
+
+    def all_pieces(buffers, slot, sems):
+        rows = pl.ds(0, (DEVS - 1) * pieces[slot][2])
+        return pltpu.make_async_copy(buffers[slot].at[rows, :], buffers[slot].at[rows, :], sems.at[slot])
+
     many = pl.ds(0, (DEVS - 1) * 8)
     for group_num in range(2):
         pltpu.make_async_copy(
@@ -289,30 +331,9 @@
         @pl.loop(0, SUB, unroll=2)
         def _(chan):
             signal_windows(chan, recv_x.at[group_num], rows_ref, win_ref)
-            convolve(group_num * SUB + chan, toep_ref, win_ref, conv_ref)
-
-    for tile in range(8):
-        turned = conv_ref[tile].T
-        for peer in range(8):
-            for quarter in range(4):
-                place = 32 * tile + 4 * peer
-                row = 16 * peer + 4 * quarter
-                send_y[quarter, place:place + 4, :] = turned[row:row + 4, :]
-    own_rows = pl.ds(pl.multiple_of(me * 4, 4), 4)
-    for quarter in range(4):
-        recv_y[quarter, own_rows, :] = send_y[quarter, own_rows, :]
-
-        @pl.loop(1, DEVS)
-        def _(step):
-            peer = lax.rem(me + step, DEVS)
-            pltpu.make_async_remote_copy(
-                src_ref=send_y.at[quarter, pl.ds(pl.multiple_of(peer * 4, 4), 4), :],
-                dst_ref=recv_y.at[quarter, own_rows, :],
-                send_sem=y_send_sem.at[quarter],
-                recv_sem=y_recv_sem.at[quarter],
-                device_id={"seq": peer},
-                device_id_type=MESH,
-            ).start()
+            convolve(group_num * SUB + chan, chan, toep_ref, win_ref, conv_ref.at[group_num])
+
+        return_rows(group_num)
 
     def to_core(quarter, which):
         return pltpu.make_async_remote_copy(
@@ -335,26 +356,30 @@
 
     for load in loads:
         load.wait()
-    part_rows = pl.ds(0, (DEVS - 1) * 4)
     first_half = iota((16, 128), 1) < 64
     for quarter in range(4):
-        pltpu.make_async_copy(
-            recv_y.at[quarter, part_rows, :], recv_y.at[quarter, part_rows, :], y_recv_sem.at[quarter]
-        ).wait()
-        for pair in range(2):
-            both = jnp.concatenate(
-                [recv_y[quarter, pl.ds(2 * pair + side, DEVS, stride=4), :] for side in range(2)], axis=0
-            ).T
+        if quarter == 0:
+            all_pieces(incoming, 0, y_recv_sem).wait()
+        if quarter < 2:
+            all_pieces(incoming, quarter + 1, y_recv_sem).wait()
+        for row in range(2):
+            if quarter == 0:
+                late = recv_y1[pl.ds(row, DEVS, stride=2), :]
+            else:
+                late = recv_y2[pl.ds(2 * (quarter - 1) + row, DEVS, stride=6), :]
+            both = jnp.concatenate([recv_y0[pl.ds(2 * quarter + row, DEVS, stride=8), :], late], axis=0).T
             swapped = pltpu.roll(both, 64, 1)
-            for two in range(OWN // 2):
-                low = slice(32 * two, 32 * two + 16)
-                high = slice(32 * two + 16, 32 * two + 32)
-                lanes = slice(128 * two, 128 * (two + 1))
-                for side, value in enumerate((
-                    jnp.where(first_half, both[low], swapped[high]), jnp.where(first_half, swapped[low], both[high])
-                )):
-                    place = 16 * (2 * pair + side)
-                    rows = slice(64 * quarter + place, 64 * quarter + place + 16)
+            for odd in range(2):
+                place = 16 * (2 * row + odd)
+                rows = slice(64 * quarter + place, 64 * quarter + place + 16)
+                for two in range(OWN // 2):
+                    left = 64 * odd + 32 * (two % 2)
+                    low, high = slice(left, left + 16), slice(left + 16, left + 32)
+                    lanes = slice(128 * two, 128 * (two + 1))
+                    if two < 2:
+                        value = jnp.where(first_half, both[low], swapped[high])
+                    else:
+                        value = jnp.where(first_half, swapped[low], both[high])
                     gated_ref[place:place + 16, lanes] = (
                         gate_ref[rows, lanes].astype(F32)
                         * (value + skip_ref[:, lanes] * sig_ref[rows, lanes].astype(F32))
@@ -380,10 +405,9 @@
         pltpu.make_async_copy(
             send_x.at[group_num, many, :], send_x.at[group_num, many, :], x_send_sem.at[group_num]
         ).wait()
+    for slot in range(3):
+        all_pieces(outgoing, slot, y_send_sem).wait()
     for quarter in range(4):
-        pltpu.make_async_copy(
-            send_y.at[quarter, part_rows, :], send_y.at[quarter, part_rows, :], y_send_sem.at[quarter]
-        ).wait()
         for which in range(2):
             to_core(quarter, which).wait_send()
         to_far(quarter).wait_send()
@@ -408,11 +432,16 @@
             pltpu.VMEM((OWN, SEQ_LEN // DEPTH * TAP, DEPTH), BF16),
             pltpu.VMEM((1088, 128), F32),
             pltpu.VMEM((1072, 256), BF16),
-            pltpu.VMEM((8, 128, 128), F32),
+            pltpu.VMEM((2, 8, SUB * TAP, 128), F32),
             pltpu.VMEM((2, DEVS * 8, 128), F32),
             pltpu.VMEM((2, DEVS * 8 + 8, 128), F32),
-            pltpu.VMEM((4, DEVS * 4, 128), F32),
-            pltpu.VMEM((4, DEVS * 4, 128), F32),
+            pltpu.VMEM((8, 128, 128), F32),
+            pltpu.VMEM((DEVS * 8, 128), F32),
+            pltpu.VMEM((DEVS * 2, 128), F32),
+            pltpu.VMEM((DEVS * 6, 128), F32),
+            pltpu.VMEM((DEVS * 8, 128), F32),
+            pltpu.VMEM((DEVS * 2, 128), F32),
+            pltpu.VMEM((DEVS * 6, 128), F32),
             pltpu.VMEM((64, CHANS), BF16),
             pltpu.VMEM((4, CHANS, COLS), BF16),
             pltpu.VMEM((4, 64, COLS), F32),

time: 71.4 us -> 70.9 us (level)
  no operation moved by 1% of the time
where the time goes in v5:
time: 70.9 us; the launch traced here: 70.8 us
  Pallas kernels  68.9 us (97%)
  local copies, waits for them, and re-layouts  1.87 us (3%)
    pallas_call x1, Pallas kernels, shards(): pl.pallas_call(block_kernel, out_shape=jax.ShapeDtypeStruct((ROWS, COLS),...  68.9 us
    unnamed x1, local copies, waits for them, and re-layouts  1.87 us

profile of v5, /device:TPU:1, one launch (start us, length us, event | category | flops | bytes accessed | tf_op | source)
XLA Modules:
  0.0 70.8 jit_solution(284367289167416673)
XLA Ops:
  0.0 68.9 %hyena_block.1 = bf16[256,1024]{1,0:T(8,128)(2,1)} custom-call(bf16[256,512]{1,0:T(8,128)(2,1)} %sig_ref.1, bf16[256,512]{1,0:T(8,128)(2,1)} %gate_ref.1, f32[1,512]{1,0:T(1,128)} %bitcast.4, f32[1,512]{1,0:T(1,128)} %bitcast.5, f32[33,64]{1,0:T(8,128)} %w1_ref.1, f32[1,64]{1,0:T(1,128)} %bitcast.6, f32[64,64]{1,0:T(8,128)} %w2_ref.1, f32[1,64]{1,0:T(1,128)} %bitcast.7, ...), custom_call_target="tpu_custom_call" | custom-call | tf_op jit(solution)/shard_map/hyena_block/pallas_call | solution.py:420
  68.9 1.9 %copy.13 = bf16[256,1024]{1,0:T(8,128)(2,1)} copy(bf16[256,1024]{1,0:T(8,128)(2,1)} %hyena_block.1) | data formatting | bytes 1048576

commit v6 on v5

--- a/solution.py
+++ b/solution.py
@@ -17,6 +17,7 @@
 CHANS = 512
 OWN = 8
 SUB = 4
+GROUPS = ((0, 4), (4, 2), (6, 2))
 HID = 64
 PARTS = 4
 QUARTER = SEQ_LEN // PARTS
@@ -171,10 +172,10 @@
     lax.fori_loop(0, SEQ_LEN // DEPTH, block, slanted(PARTS - 1, per_part - 1))
 
 
-def signal_windows(chan, recv_ref, rows_ref, win_ref):
+def signal_windows(chan, count, recv_ref, rows_ref, win_ref):
     lane = iota((128, 128), 1)
-    before = recv_ref[pl.ds(SUB + chan, 128, stride=SUB), :]
-    after = recv_ref[pl.ds(2 * SUB + chan, 128, stride=SUB), :]
+    before = recv_ref[pl.ds(8 - count + chan, 128, stride=count), :]
+    after = recv_ref[pl.ds(8 + chan, 128, stride=count), :]
     for sub in range(8):
         ahead = TAP * (sub + 1)
         value = after
@@ -213,7 +214,7 @@
 def block_kernel(sig_ref, gate_ref, skip_ref, decay_ref, w1_ref, b1_ref, w2_ref, b2_ref, hi_ref, fix_ref, wout_ref,
                  out_ref,
                  first_ref, second_ref, bias_ref, third_ref, env_ref, filt_ref, toep_ref, rows_ref, win_ref, conv_ref,
-                 send_x, recv_x, turn_ref, send_y0, send_y1, send_y2, recv_y0, recv_y1, recv_y2, gated_ref, wide_ref, total_ref, mixed_ref,
+                 send_x0, send_x1, send_x2, recv_x0, recv_x1, recv_x2, turn_ref, send_y0, send_y1, send_y2, recv_y0, recv_y1, recv_y2, gated_ref, wide_ref, total_ref, mixed_ref,
                  core_send, core_recv, far_send, far_recv,
                  wide_sem, x_send_sem, x_recv_sem, y_send_sem, y_recv_sem,
                  core_send_sem, core_recv_sem, far_send_sem, far_recv_sem, out_sem):
@@ -243,31 +244,34 @@
     for load in loads:
         load.start()
 
+    leaving, landing = (send_x0, send_x1, send_x2), (recv_x0, recv_x1, recv_x2)
     for half in range(2):
         turned = sig_ref[128 * half:128 * (half + 1), :].astype(F32).T
-        for chan in range(OWN):
-            send_x[chan // SUB, pl.ds(SUB * half + chan % SUB, DEVS, stride=8), :] = (
-                turned[DEVS * chan:DEVS * (chan + 1), :]
-            )
-    own_send = pl.ds(pl.multiple_of(me * 8, 8), 8)
-    own_recv = pl.ds(pl.multiple_of(me * 8 + 8, 8), 8)
-    for group_num in range(2):
-        recv_x[group_num, 0:8, :] = jnp.zeros((8, 128), F32)
-        recv_x[group_num, own_recv, :] = send_x[group_num, own_send, :]
+        for slot, (first, count) in enumerate(GROUPS):
+            for chan in range(count):
+                place = DEVS * (first + chan)
+                leaving[slot][pl.ds(count * half + chan, DEVS, stride=2 * count), :] = turned[place:place + DEVS, :]
+
+    def block_rows(device, count, offset=0):
+        return pl.ds(pl.multiple_of(device * (2 * count) + offset, 4), 2 * count)
+
+    for slot, (_, count) in enumerate(GROUPS):
+        landing[slot][0:8, :] = jnp.zeros((8, 128), F32)
+        landing[slot][block_rows(me, count, 8), :] = leaving[slot][block_rows(me, count), :]
     filter_weights(me, decay_ref, w1_ref, b1_ref, w2_ref, b2_ref, hi_ref, fix_ref,
                    first_ref, second_ref, bias_ref, third_ref, env_ref)
     pl.semaphore_wait(barrier, DEVS + 1)
 
-    for group_num in range(2):
+    for slot, (_, count) in enumerate(GROUPS):
 
         @pl.loop(1, DEVS)
         def _(step):
             peer = lax.rem(me + step, DEVS)
             pltpu.make_async_remote_copy(
-                src_ref=send_x.at[group_num, pl.ds(pl.multiple_of(peer * 8, 8), 8), :],
-                dst_ref=recv_x.at[group_num, own_recv, :],
-                send_sem=x_send_sem.at[group_num],
-                recv_sem=x_recv_sem.at[group_num],
+                src_ref=leaving[slot].at[block_rows(peer, count), :],
+                dst_ref=landing[slot].at[block_rows(me, count, 8), :],
+                send_sem=x_send_sem.at[slot],
+                recv_sem=x_recv_sem.at[slot],
                 device_id={"seq": peer},
                 device_id_type=MESH,
             ).start()
@@ -306,9 +310,7 @@
             if which == group_num:
                 incoming[slot][own_piece(size), :] = outgoing[slot][own_piece(size), :]
 
-                @pl.loop(1, DEVS)
-                def _(step):
-                    peer = lax.rem(me + step, DEVS)
+                def send_piece(peer):
                     pltpu.make_async_remote_copy(
                         src_ref=outgoing[slot].at[pl.ds(pl.multiple_of(peer * size, 2), size), :],
                         dst_ref=incoming[slot].at[own_piece(size), :],
@@ -318,22 +320,34 @@
                         device_id_type=MESH,
                     ).start()
 
+                x_half = lax.div(me, DEVS // 2)
+
+                @pl.loop(0, DEVS // 2)
+                def _(step):
+                    send_piece((1 - x_half) * (DEVS // 2) + lax.rem(me + step, DEVS // 2))
+
+                @pl.loop(1, DEVS // 2)
+                def _(step):
+                    send_piece(x_half * (DEVS // 2) + lax.rem(me + step, DEVS // 2))
+
     def all_pieces(buffers, slot, sems):
         rows = pl.ds(0, (DEVS - 1) * pieces[slot][2])
         return pltpu.make_async_copy(buffers[slot].at[rows, :], buffers[slot].at[rows, :], sems.at[slot])
 
-    many = pl.ds(0, (DEVS - 1) * 8)
-    for group_num in range(2):
-        pltpu.make_async_copy(
-            recv_x.at[group_num, many, :], recv_x.at[group_num, many, :], x_recv_sem.at[group_num]
-        ).wait()
-
-        @pl.loop(0, SUB, unroll=2)
+    def all_blocks(buffers, slot, sems):
+        rows = pl.ds(0, (DEVS - 1) * 2 * GROUPS[slot][1])
+        return pltpu.make_async_copy(buffers[slot].at[rows, :], buffers[slot].at[rows, :], sems.at[slot])
+
+    for slot, (first, count) in enumerate(GROUPS):
+        all_blocks(landing, slot, x_recv_sem).wait()
+
+        @pl.loop(0, count, unroll=2)
         def _(chan):
-            signal_windows(chan, recv_x.at[group_num], rows_ref, win_ref)
-            convolve(group_num * SUB + chan, chan, toep_ref, win_ref, conv_ref.at[group_num])
-
-        return_rows(group_num)
+            signal_windows(chan, count, landing[slot], rows_ref, win_ref)
+            convolve(first + chan, first % SUB + chan, toep_ref, win_ref, conv_ref.at[first // SUB])
+
+        if (first + count) % SUB == 0:
+            return_rows(first // SUB)
 
     def to_core(quarter, which):
         return pltpu.make_async_remote_copy(
@@ -401,10 +415,8 @@
     for quarter in range(4):
         to_out(quarter).wait()
 
-    for group_num in range(2):
-        pltpu.make_async_copy(
-            send_x.at[group_num, many, :], send_x.at[group_num, many, :], x_send_sem.at[group_num]
-        ).wait()
+    for slot in range(3):
+        all_blocks(leaving, slot, x_send_sem).wait()
     for slot in range(3):
         all_pieces(outgoing, slot, y_send_sem).wait()
     for quarter in range(4):
@@ -433,8 +445,12 @@
             pltpu.VMEM((1088, 128), F32),
             pltpu.VMEM((1072, 256), BF16),
             pltpu.VMEM((2, 8, SUB * TAP, 128), F32),
-            pltpu.VMEM((2, DEVS * 8, 128), F32),
-            pltpu.VMEM((2, DEVS * 8 + 8, 128), F32),
+            pltpu.VMEM((DEVS * 8, 128), F32),
+            pltpu.VMEM((DEVS * 4, 128), F32),
+            pltpu.VMEM((DEVS * 4, 128), F32),
+            pltpu.VMEM((DEVS * 8 + 8, 128), F32),
+            pltpu.VMEM((DEVS * 4 + 8, 128), F32),
+            pltpu.VMEM((DEVS * 4 + 8, 128), F32),
             pltpu.VMEM((8, 128, 128), F32),
             pltpu.VMEM((DEVS * 8, 128), F32),
             pltpu.VMEM((DEVS * 2, 128), F32),
@@ -451,8 +467,8 @@
             pltpu.VMEM((4, 64, COLS), F32),
             pltpu.VMEM((4, 64, COLS), F32),
             pltpu.SemaphoreType.DMA((4,)),
-            pltpu.SemaphoreType.DMA((2,)),
-            pltpu.SemaphoreType.DMA((2,)),
+            pltpu.SemaphoreType.DMA((3,)),
+            pltpu.SemaphoreType.DMA((3,)),
             pltpu.SemaphoreType.DMA((4,)),
             pltpu.SemaphoreType.DMA((4,)),
             pltpu.SemaphoreType.DMA((4, 2)),

time: 70.9 us -> 71.8 us (1.013)
  Pallas kernels: 68.9 us -> 69.8 us
    pallas_call x1, Pallas kernels: 68.9 us -> 69.8 us  [shards(): pl.pallas_call(block_kernel, out_shape=jax.ShapeDtypeStruct((ROWS, COLS),...]
where the time goes in v6:
time: 71.8 us; the launch traced here: 71.6 us
  Pallas kernels  69.8 us (97%)
  local copies, waits for them, and re-layouts  1.87 us (3%)
    pallas_call x1, Pallas kernels, shards(): pl.pallas_call(block_kernel, out_shape=jax.ShapeDtypeStruct((ROWS, COLS),...  69.8 us
    unnamed x1, local copies, waits for them, and re-layouts  1.87 us

profile of v6, /device:TPU:1, one launch (start us, length us, event | category | flops | bytes accessed | tf_op | source)
XLA Modules:
  0.0 71.6 jit_solution(12421628052550684352)
XLA Ops:
  0.0 69.8 %hyena_block.1 = bf16[256,1024]{1,0:T(8,128)(2,1)} custom-call(bf16[256,512]{1,0:T(8,128)(2,1)} %sig_ref.1, bf16[256,512]{1,0:T(8,128)(2,1)} %gate_ref.1, f32[1,512]{1,0:T(1,128)} %bitcast.4, f32[1,512]{1,0:T(1,128)} %bitcast.5, f32[33,64]{1,0:T(8,128)} %w1_ref.1, f32[1,64]{1,0:T(1,128)} %bitcast.6, f32[64,64]{1,0:T(8,128)} %w2_ref.1, f32[1,64]{1,0:T(1,128)} %bitcast.7, ...), custom_call_target="tpu_custom_call" | custom-call | tf_op jit(solution)/shard_map/hyena_block/pallas_call | solution.py:432
  69.8 1.9 %copy.13 = bf16[256,1024]{1,0:T(8,128)(2,1)} copy(bf16[256,1024]{1,0:T(8,128)(2,1)} %hyena_block.1) | data formatting | bytes 1048576

commit v7 on v5

--- a/solution.py
+++ b/solution.py
@@ -256,6 +256,10 @@
         recv_x[group_num, own_recv, :] = send_x[group_num, own_send, :]
     filter_weights(me, decay_ref, w1_ref, b1_ref, w2_ref, b2_ref, hi_ref, fix_ref,
                    first_ref, second_ref, bias_ref, third_ref, env_ref)
+    @pl.loop(0, 2)
+    def _(step):
+        filter_step(step, first_ref, second_ref, bias_ref, third_ref, env_ref, filt_ref)
+
     pl.semaphore_wait(barrier, DEVS + 1)
 
     for group_num in range(2):
@@ -272,7 +276,7 @@
                 device_id_type=MESH,
             ).start()
 
-    @pl.loop(0, QUARTER // STEP)
+    @pl.loop(2, QUARTER // STEP)
     def _(step):
         filter_step(step, first_ref, second_ref, bias_ref, third_ref, env_ref, filt_ref)
 

time: 70.9 us -> 69.8 us (0.984)
  Pallas kernels: 68.9 us -> 67.8 us
    pallas_call x1, Pallas kernels: 68.9 us -> 67.8 us  [shards(): pl.pallas_call(block_kernel, out_shape=jax.ShapeDtypeStruct((ROWS, COLS),...]
where the time goes in v7:
time: 69.8 us; the launch traced here: 69.7 us
  Pallas kernels  67.8 us (97%)
  local copies, waits for them, and re-layouts  1.87 us (3%)
    pallas_call x1, Pallas kernels, shards(): pl.pallas_call(block_kernel, out_shape=jax.ShapeDtypeStruct((ROWS, COLS),...  67.8 us
    unnamed x1, local copies, waits for them, and re-layouts  1.87 us

profile of v7, /device:TPU:1, one launch (start us, length us, event | category | flops | bytes accessed | tf_op | source)
XLA Modules:
  0.0 69.7 jit_solution(14882847049626367851)
XLA Ops:
  0.0 67.8 %hyena_block.1 = bf16[256,1024]{1,0:T(8,128)(2,1)} custom-call(bf16[256,512]{1,0:T(8,128)(2,1)} %sig_ref.1, bf16[256,512]{1,0:T(8,128)(2,1)} %gate_ref.1, f32[1,512]{1,0:T(1,128)} %bitcast.4, f32[1,512]{1,0:T(1,128)} %bitcast.5, f32[33,64]{1,0:T(8,128)} %w1_ref.1, f32[1,64]{1,0:T(1,128)} %bitcast.6, f32[64,64]{1,0:T(8,128)} %w2_ref.1, f32[1,64]{1,0:T(1,128)} %bitcast.7, ...), custom_call_target="tpu_custom_call" | custom-call | tf_op jit(solution)/shard_map/hyena_block/pallas_call | solution.py:424
  67.8 1.9 %copy.13 = bf16[256,1024]{1,0:T(8,128)(2,1)} copy(bf16[256,1024]{1,0:T(8,128)(2,1)} %hyena_block.1) | data formatting | bytes 1048576

commit v8 on v7

--- a/solution.py
+++ b/solution.py
@@ -291,14 +291,15 @@
 
     def return_rows(group_num):
         even_half = iota((64, 128), 1) < 64
-        for tile in range(8):
-            value = conv_ref[group_num, tile]
-            turn_ref[tile] = jnp.concatenate([value, value], axis=0).T
-            block = jnp.where(
-                even_half, turn_ref[tile, pl.ds(0, 64, stride=2), :], turn_ref[tile, pl.ds(1, 64, stride=2), :]
-            )
-            for slot, (which, first, size) in enumerate(pieces):
-                if which == group_num:
+        for slot, (which, first, size) in enumerate(pieces):
+            if which == group_num:
+                for tile in range(8):
+                    if first == 0:
+                        value = conv_ref[group_num, tile]
+                        turn_ref[tile] = jnp.concatenate([value, value], axis=0).T
+                    block = jnp.where(
+                        even_half, turn_ref[tile, pl.ds(0, 64, stride=2), :], turn_ref[tile, pl.ds(1, 64, stride=2), :]
+                    )
                     if size == 8:
                         outgoing[slot][64 * tile:64 * (tile + 1), :] = block
                     else:
@@ -306,8 +307,6 @@
                             place = (8 * tile + peer) * size
                             row = 8 * peer + first
                             outgoing[slot][place:place + size, :] = block[row:row + size, :]
-        for slot, (which, _, size) in enumerate(pieces):
-            if which == group_num:
                 incoming[slot][own_piece(size), :] = outgoing[slot][own_piece(size), :]
 
                 @pl.loop(1, DEVS)
@@ -332,7 +331,7 @@
             recv_x.at[group_num, many, :], recv_x.at[group_num, many, :], x_recv_sem.at[group_num]
         ).wait()
 
-        @pl.loop(0, SUB, unroll=2)
+        @pl.loop(0, SUB, unroll=4)
         def _(chan):
             signal_windows(chan, recv_x.at[group_num], rows_ref, win_ref)
             convolve(group_num * SUB + chan, chan, toep_ref, win_ref, conv_ref.at[group_num])

time: 69.8 us -> 69.5 us (level)
  no operation moved by 1% of the time
where the time goes in v8:
time: 69.5 us; the launch traced here: 69.4 us
  Pallas kernels  67.5 us (97%)
  local copies, waits for them, and re-layouts  1.87 us (3%)
    pallas_call x1, Pallas kernels, shards(): pl.pallas_call(block_kernel, out_shape=jax.ShapeDtypeStruct((ROWS, COLS),...  67.5 us
    unnamed x1, local copies, waits for them, and re-layouts  1.87 us

profile of v8, /device:TPU:1, one launch (start us, length us, event | category | flops | bytes accessed | tf_op | source)
XLA Modules:
  0.0 69.4 jit_solution(1496961202585013715)
XLA Ops:
  0.0 67.5 %hyena_block.1 = bf16[256,1024]{1,0:T(8,128)(2,1)} custom-call(bf16[256,512]{1,0:T(8,128)(2,1)} %sig_ref.1, bf16[256,512]{1,0:T(8,128)(2,1)} %gate_ref.1, f32[1,512]{1,0:T(1,128)} %bitcast.4, f32[1,512]{1,0:T(1,128)} %bitcast.5, f32[33,64]{1,0:T(8,128)} %w1_ref.1, f32[1,64]{1,0:T(1,128)} %bitcast.6, f32[64,64]{1,0:T(8,128)} %w2_ref.1, f32[1,64]{1,0:T(1,128)} %bitcast.7, ...), custom_call_target="tpu_custom_call" | custom-call | tf_op jit(solution)/shard_map/hyena_block/pallas_call | solution.py:423
  67.5 1.9 %copy.13 = bf16[256,1024]{1,0:T(8,128)(2,1)} copy(bf16[256,1024]{1,0:T(8,128)(2,1)} %hyena_block.1) | data formatting | bytes 1048576
